TPU v7x, 32 devices: a whole 2x2x4 slice. The times are simulated.
32 devices in a mesh: dp: 2 (over z_hi), expert: 8 (over y, x, core), tensor: 2 (over z_lo).
Axes of the slice: x: 2, y: 2, z: 4 (z_hi: 2, z_lo: 2; z = z_hi * 2 + z_lo), core: 2. Of those that a mesh axis runs over, the one named last changes fastest.
Arguments:
- tokens: bfloat16 [2048, 2048], P(('dp', 'expert')), may hold values from -6 to 6
- expert_ids: int32 [2048, 8], P(('dp', 'expert')), may hold values from 0 to 15, all different within a row; in each aligned block of 64 rows (0 to 63, 64 to 127, ...) at most 64 rows name the same one
- weights: bfloat16 [2, 16, 768, 2048], P(None, 'expert', 'tensor'), may hold values from -0.125 to 0.125
- first_moment: bfloat16 [2, 16, 768, 2048], P('dp', 'expert', 'tensor'), may hold values from -6 to 6
- second_moment: bfloat16 [2, 16, 768, 2048], P('dp', 'expert', 'tensor'), may hold values from 1 to 100
- hidden_grad: bfloat16 [2, 16, 768, 1024], P('dp', 'expert', 'tensor'), may hold values from -6 to 6
- swap_list: int32 [4, 2], replicated, may hold values from 0 to 15, as said below
Outputs:
- hidden: bfloat16 [2, 16, 768, 1024], P('dp', 'expert', 'tensor')
- token_grad: bfloat16 [2048, 2048], P(('dp', 'expert', 'tensor'))
- new_weights: bfloat16 [2, 16, 768, 2048], P('dp', 'expert', 'tensor')
- new_first: bfloat16 [2, 16, 768, 2048], P('dp', 'expert', 'tensor')
- new_second: bfloat16 [2, 16, 768, 2048], P('dp', 'expert', 'tensor')
Inputs may be any that keep to these rules, and one draw needn't show every extreme that they name: `expert_ids`: each row names 8 different experts. Within the rows of one quarter block of 64 rows no expert is named by more than 64 rows, a bound that some block reaches. `swap_list`: expert e is owned by index e // 2 of expert. The owners of the two experts of a row are 4 indices apart, and no owner appears in two rows.
All inputs are finite; a program needn't handle non-finite values.
Results may differ from a plain program's by a relative error of at most 0.0065.
Values may be sent and summed in bfloat16 or wider, within the bound.
No kernel may reach another device: no remote copies, remote signals or barrier semaphores. Data moves between devices by JAX's collectives and lax.ppermute only.
A program may use at most 192 MiB of HBM per device.

v0:
```python
import jax
import jax.numpy as jnp
from jax import lax
from jax.sharding import PartitionSpec as P

beta_one = 0.9
beta_two = 0.95
step_size = 0.01
adam_eps = 1e-08


def partner(value, axis, bit):
    return lax.ppermute(value, axis, [(i, i ^ 1 << bit) for i in range(lax.axis_size(axis))])


def slot_select(expert_ids, blocks, per_dev, owners, capacity):
    row_total = expert_ids.shape[0]
    top_count = expert_ids.shape[1]
    pair_total = row_total * top_count
    block_pairs = pair_total // blocks
    expert_total = per_dev * owners
    named_flat = expert_ids.reshape(blocks, block_pairs)
    one_hot = (
        named_flat[:, :, None] == jnp.arange(expert_total, dtype=jnp.int32)[None, None, :]
    ).astype(jnp.int32)
    slot_rank = (jnp.sum(jnp.cumsum(one_hot, axis=1) * one_hot, axis=2) - 1).reshape(pair_total)
    block_index = jnp.arange(pair_total, dtype=jnp.int32) // block_pairs
    expert_flat = named_flat.reshape(pair_total)
    slot_key = (
        (expert_flat % per_dev * owners + expert_flat // per_dev) * blocks + block_index
    ) * capacity + slot_rank
    key_total = expert_total * blocks * capacity
    by_key = (jnp.arange(key_total, dtype=jnp.int32)[:, None] == slot_key[None, :]).astype(
        jnp.bfloat16
    )
    pair_rows = jnp.arange(pair_total, dtype=jnp.int32) // top_count
    by_row = (pair_rows[:, None] == jnp.arange(row_total, dtype=jnp.int32)[None, :]).astype(
        jnp.bfloat16
    )
    return jnp.dot(by_key, by_row, preferred_element_type=jnp.float32).astype(jnp.bfloat16)


def migration_slot(swap_list, per_dev):
    own_index = lax.axis_index("expert")
    first_hit = swap_list[:, 0] // per_dev == own_index
    second_hit = swap_list[:, 1] // per_dev == own_index
    chosen = jnp.sum(
        jnp.where(first_hit, swap_list[:, 0] % per_dev, 0)
        + jnp.where(second_hit, swap_list[:, 1] % per_dev, 0)
    )
    return (chosen, jnp.any(first_hit | second_hit))


def pick_slot(state, chosen):
    return lax.dynamic_index_in_dim(state, chosen, 1, keepdims=False)


def place_slot(state, incoming, chosen, moving):
    target = (jnp.arange(state.shape[1], dtype=jnp.int32) == chosen) & moving
    return jnp.where(target[None, :, None, None], incoming[:, None], state)


def adam_step(weight_half, first_moment, second_moment, weight_grad):
    first_next = beta_one * first_moment.astype(jnp.float32) + (1.0 - beta_one) * weight_grad
    second_next = (
        beta_two * second_moment.astype(jnp.float32) + (1.0 - beta_two) * weight_grad * weight_grad
    )
    updated = weight_half.astype(jnp.float32) - step_size * first_next / (
        jnp.sqrt(second_next) + adam_eps
    )
    return (
        updated.astype(jnp.bfloat16),
        first_next.astype(jnp.bfloat16),
        second_next.astype(jnp.bfloat16),
    )


def shards(tokens, expert_ids, weights, first_moment, second_moment, hidden_grad, swap_list):
    owners = lax.axis_size("expert")
    tensor_count = lax.axis_size("tensor")
    replicas = lax.axis_size("dp")
    per_dev = weights.shape[1]
    model_width = tokens.shape[1]
    slots_total = hidden_grad.shape[3]
    capacity = slots_total // (owners * tensor_count)
    quarter_rows = tokens.shape[0] // tensor_count
    quarter_index = lax.axis_index("tensor")
    whole_select = slot_select(expert_ids, tensor_count, per_dev, owners, capacity)
    outgoing = jnp.dot(whole_select, tokens, preferred_element_type=jnp.float32).astype(
        jnp.bfloat16
    )
    outgoing = outgoing.reshape(per_dev, owners, tensor_count * capacity, model_width)
    arrived = lax.all_to_all(outgoing, "expert", split_axis=1, concat_axis=1, tiled=True)
    select_grid = whole_select.reshape(
        per_dev, owners, tensor_count, capacity, tensor_count, quarter_rows
    )
    select_grid = lax.dynamic_index_in_dim(select_grid, quarter_index, 2, keepdims=False)
    select_grid = lax.dynamic_index_in_dim(select_grid, quarter_index, 3, keepdims=False)
    own_select = select_grid.reshape(per_dev * owners * capacity, quarter_rows)
    routed = arrived.reshape(per_dev, slots_total, model_width)
    half_rows = 2 // replicas
    replica_index = lax.axis_index("dp")
    weight_half = lax.dynamic_slice_in_dim(weights, replica_index * half_rows, half_rows, 0)
    chosen, moving = migration_slot(swap_list, per_dev)
    top_bit = owners.bit_length() - 2
    projected = jnp.einsum("cefd,esd->ecfs", weights, routed, preferred_element_type=jnp.float32)
    gate_pre = projected[:, 0]
    up_pre = projected[:, 1]
    sigmoid_gate = jax.nn.sigmoid(gate_pre)
    hidden = (gate_pre * sigmoid_gate * up_pre).astype(jnp.bfloat16)
    grad_hidden = hidden_grad[0].astype(jnp.float32)
    grad_gate = grad_hidden * up_pre * sigmoid_gate * (1.0 + gate_pre * (1.0 - sigmoid_gate))
    grad_up = grad_hidden * gate_pre * sigmoid_gate
    grad_pre = jnp.stack([grad_gate, grad_up], axis=1).astype(jnp.bfloat16)
    slot_terms = jnp.einsum("ecfs,cefd->esd", grad_pre, weights, preferred_element_type=jnp.float32)
    slot_terms = slot_terms.reshape(per_dev, owners, tensor_count, capacity, model_width)
    summed = lax.psum_scatter(
        slot_terms.astype(jnp.bfloat16), "tensor", scatter_dimension=2, tiled=True
    )
    returning = summed.reshape(per_dev, owners, capacity, model_width)
    back_rows = lax.all_to_all(returning, "expert", split_axis=1, concat_axis=1, tiled=True)
    token_grad = jnp.dot(
        own_select.T,
        back_rows.reshape(per_dev * owners * capacity, model_width),
        preferred_element_type=jnp.float32,
    ).astype(jnp.bfloat16)

    def grad_rows(offset, number):
        part_grad = lax.dynamic_slice_in_dim(grad_pre, offset, number, 1)
        return jnp.einsum("esd,ecfs->cefd", routed, part_grad, preferred_element_type=jnp.float32)

    own_term = grad_rows(replica_index * half_rows, half_rows)
    other_term = grad_rows((1 - replica_index) * half_rows, half_rows)
    weight_grad = own_term + partner(other_term, "dp", 0)
    updated, first_next, second_next = adam_step(
        weight_half, first_moment, second_moment, weight_grad
    )
    arrived_states = partner(
        (pick_slot(updated, chosen), pick_slot(first_next, chosen), pick_slot(second_next, chosen)),
        "expert",
        top_bit,
    )
    new_weights = place_slot(updated, arrived_states[0], chosen, moving)
    new_first = place_slot(first_next, arrived_states[1], chosen, moving)
    new_second = place_slot(second_next, arrived_states[2], chosen, moving)
    return (hidden[None], token_grad, new_weights, new_first, new_second)


def solution(mesh):
    in_specs = (
        P(("dp", "expert"), None),
        P(("dp", "expert"), None),
        P(None, "expert", "tensor", None),
        P("dp", "expert", "tensor", None),
        P("dp", "expert", "tensor", None),
        P("dp", "expert", "tensor", None),
        P(),
    )
    out_specs = (
        P("dp", "expert", "tensor", None),
        P(("dp", "expert", "tensor"), None),
        P("dp", "expert", "tensor", None),
        P("dp", "expert", "tensor", None),
        P("dp", "expert", "tensor", None),
    )
    return jax.shard_map(shards, mesh=mesh, in_specs=in_specs, out_specs=out_specs, check_vma=False)
```

profile of v0, /device:TPU:0, one launch (start us, length us, event | category | flops | bytes accessed | tf_op | source)
XLA Modules:
  0.0 667.6 jit_solution(12819132871745916266)
XLA Ops:
  7.2 0.8 copy.41
  8.0 0.1 eq.85
  8.1 0.1 eq.81
  8.2 0.1 reshape_reshape.3
  8.3 2.3 reduce-window.6
  10.6 0.3 slice_reduce_fusion
  11.0 0.1 fusion.29
  11.1 1.6 fusion.20
  12.8 5.6 convolution_convert_fusion
  18.3 8.3 %copy.45 = bf16[2,8,128,2048]{3,2,0,1:T(8,128)(2,1)} copy(bf16[2,8,128,2048]{3,2,1,0:T(8,128)(2,1)} %bitcast.124) | data formatting | bytes 16777216 | tf_op jit(solution)/shard_map/reshape | solution.py:92
  26.6 5.2 all-to-all-start
  31.8 0.2 all-reduce.3.cloned.1.call-start
  32.0 1.9 copy.49
  33.9 92.4 %all-to-all-done = bf16[2,8,128,2048]{3,2,0,1:T(8,128)(2,1)} async-done(((bf16[2,8,128,2048]{3,2,0,1:T(8,128)(2,1)}), bf16[2,8,128,2048]{3,2,0,1:T(8,128)(2,1)}, u32[]{:S(2)}, u32[]{:S(2)}) %all-to-all-start) | async-done | bytes 8388640 | tf_op jit(solution)/shard_map/all_to_all | solution.py:93
  126.3 8.4 %copy.46 = bf16[2,8,128,2048]{3,2,1,0:T(8,128)(2,1)} copy(bf16[2,8,128,2048]{3,2,0,1:T(8,128)(2,1)} %all-to-all-done) | data formatting | bytes 16777216 | tf_op jit(solution)/shard_map/all_to_all | solution.py:93
  134.7 10.2 %fusion.17 = f32[2,2,384,1024]{2,3,1,0:T(8,128)S(1)} fusion(bf16[2,1024,2048,1]{2,1,3,0:T(8,128)(2,1)} %bitcast.126, bf16[2,2,384,2048]{3,2,1,0:T(8,128)(2,1)} %param.9), kind=kOutput, calls=%fused_computation.40 | convolution fusion | flops 6442450944 | bytes 20971520 | tf_op jit(solution)/shard_map/cefd,esd->ecfs/dot_general | solution.py:106
  145.0 1.6 fusion.10
  146.6 1.1 copy-done.2
  147.7 8.9 %bitcast_convert_fusion = bf16[2,1024,2048]{2,1,0:T(8,128)(2,1)} fusion(bf16[2,2,384,2048]{3,2,1,0:T(8,128)(2,1)S(1)} %bitcast.133, bf16[2,1,384,1024]{2,3,1,0:T(8,128)(2,1)S(1)} %get-tuple-element.32, bf16[2,1,384,1024]{2,3,1,0:T(8,128)(2,1)S(1)} %get-tuple-element.31), kind=kOutput, calls=%fused_computation | convolution fusion | flops 6448218112 | bytes 17825792 | tf_op jit(solution)/shard_map/ecfs,cefd->esd/dot_general | solution.py:115
  156.6 1.4 copy-done.7
  158.0 10.1 %convolution_bitcast_fusion = f32[1,2,384,2048]{3,2,1,0:T(8,128)} fusion(bf16[2,1024,2048]{2,1,0:T(8,128)(2,1)} %bitcast.127, s32[]{:T(128)S(6)} %select_n.103, bf16[2,1,384,1024]{2,3,1,0:T(8,128)(2,1)S(1)} %copy-done.7, bf16[2,1,384,1024]{2,3,1,0:T(8,128)(2,1)} %copy-done.8), kind=kOutput, calls=%fused_computation.21 | convolution fusion | flops 3222011904 | bytes 17825796 | tf_op jit(solution)/shard_map/esd,ecfs->cefd/dot_general | solution.py:130
  168.1 3.0 collective-permute-start
  171.0 0.6 fusion.49
  173.0 0.6 dynamic-slice.2
  174.2 313.7 %all-reduce.3.cloned.1.call-done = bf16[2,8,2,64,2048]{4,3,2,1,0:T(8,128)(2,1)} async-done(((bf16[2,8,2,64,2048]{4,3,2,1,0:T(8,128)(2,1)}), bf16[2,8,2,64,2048]{4,3,2,1,0:T(8,128)(2,1)}) %all-reduce.3.cloned.1.call-update) | async-done | bytes 8388624
  487.9 3.1 dynamic-slice_bitcast_fusion
  491.0 2.2 copy.51
  493.3 4.8 all-to-all-start.1
  498.1 14.1 %fusion.7 = (bf16[1,2,384,2048]{3,2,1,0:T(8,128)(2,1)S(1)}, bf16[1,2,384,2048]{3,2,1,0:T(8,128)(2,1)S(1)}, bf16[1,2,384,2048]{3,2,1,0:T(8,128)(2,1)}) fusion(bf16[1,2,384,2048]{3,2,1,0:T(8,128)(2,1)} %param.11, bf16[1,2,384,2048]{3,2,1,0:T(8,128)(2,1)} %param.10, bf16[2,2,384,2048]{3,2,1,0:T(8,128)(2,1)} %param.9, s32[]{:T(128)S(6)} %select_n.102, ...), kind=kOutput, calls=%fused_computation.23 | convolution fusion | flops 3250323456 | bytes 36701184 | tf_op jit(solution)/shard_map/esd,ecfs->cefd/dot_general | solution.py:130
  512.2 1.3 dynamic-slice_bitcast_fusion.1
  513.6 1.4 dynamic-slice_bitcast_fusion.3
  514.9 0.4 copy-done.3
  515.3 1.1 copy-done.4
  516.4 1.3 dynamic-slice_bitcast_fusion.2
  517.6 2.0 collective-permute-start.2
  519.7 2.0 collective-permute-start.3
  521.6 0.4 reshape.219
  522.0 0.6 constant_dynamic-slice_fusion
  522.7 0.6 or_reduce_fusion
  523.3 1.3 compare_and_fusion
  524.6 3.7 fusion.13
  528.4 1.6 copy.55
  530.0 50.6 %collective-permute-done.2 = bf16[1,384,2048]{2,1,0:T(8,128)(2,1)} collective-permute-done((bf16[1,384,2048]{2,1,0:T(8,128)(2,1)}, bf16[1,384,2048]{2,1,0:T(8,128)(2,1)}, u32[]{:S(2)}, u32[]{:S(2)}) %collective-permute-start.2) | collective-permute-done | bytes 1572896 | tf_op jit(solution)/shard_map/ppermute | solution.py:13
  580.6 33.7 %collective-permute-done.1 = bf16[1,384,2048]{2,1,0:T(8,128)(2,1)} collective-permute-done((bf16[1,384,2048]{2,1,0:T(8,128)(2,1)}, bf16[1,384,2048]{2,1,0:T(8,128)(2,1)}, u32[]{:S(2)}, u32[]{:S(2)}) %collective-permute-start.1) | collective-permute-done | bytes 1572896 | tf_op jit(solution)/shard_map/ppermute | solution.py:13
  614.3 33.1 %collective-permute-done.3 = bf16[1,384,2048]{2,1,0:T(8,128)(2,1)} collective-permute-done((bf16[1,384,2048]{2,1,0:T(8,128)(2,1)}, bf16[1,384,2048]{2,1,0:T(8,128)(2,1)}, u32[]{:S(2)}, u32[]{:S(2)}) %collective-permute-start.3) | collective-permute-done | bytes 1572896 | tf_op jit(solution)/shard_map/ppermute | solution.py:13
  647.4 9.1 %broadcast_select_fusion = (bf16[1,2,384,2048]{3,2,1,0:T(8,128)(2,1)}, bf16[1,2,384,2048]{3,2,1,0:T(8,128)(2,1)}, bf16[1,2,384,2048]{3,2,1,0:T(8,128)(2,1)}) fusion(bf16[1,2,384,2048]{3,2,1,0:T(8,128)(2,1)} %copy-done.3, pred[2]{0:T(512)(128)(4,1)S(1)} %compare_and_fusion, bf16[384,2048]{1,0:T(8,128)(2,1)} %bitcast.26, ...), kind=kLoop, calls=%fused_computation.37 | loop fusion | flops 4718592 | bytes 23592962 | tf_op jit(solution)/shard_map/jit(_where)/select_n | solution.py:60
  656.6 2.6 copy.52
  659.1 1.6 convolution_convert_fusion.1
  (34 shorter events, 0.3 us)
Async XLA Ops:
  7.2 5.6 copy-start
  26.6 99.7 %all-to-all-start = ((bf16[2,8,128,2048]{3,2,0,1:T(8,128)(2,1)}), bf16[2,8,128,2048]{3,2,0,1:T(8,128)(2,1)}, u32[]{:S(2)}, u32[]{:S(2)}) async-start(bf16[2,8,128,2048]{3,2,0,1:T(8,128)(2,1)} %copy.45), calls=%async_computation | async-start | bytes 16777216 | tf_op jit(solution)/shard_map/all_to_all | solution.py:93
  31.8 456.1 %all-reduce.3.cloned.1.call-start = ((), (), s32[]{:S(2)}) async-start(), calls=%async_computation.2 | async-start | bytes 16777216
  126.3 21.4 %slice-start = ((s8[6291456]{0:T(1024)(128)(4,1)}), s8[2097152]{0:T(1024)(128)(4,1)S(1)}, s32[]{:S(2)}) async-start(s8[6291456]{0:T(1024)(128)(4,1)} %bitcast.132), calls=%async_computation.3 | async-start | bytes 4194304
  134.7 12.9 %slice-start.1 = ((s8[6291456]{0:T(1024)(128)(4,1)}), s8[4194304]{0:T(1024)(128)(4,1)S(1)}, s32[]{:S(2)}) async-start(s8[6291456]{0:T(1024)(128)(4,1)} %bitcast.132), calls=%async_computation.4 | async-start | bytes 8388608
  145.0 2.7 copy-start.2
  147.7 8.9 %copy-start.6 = (bf16[2,1,384,1024]{2,3,1,0:T(8,128)(2,1)}, bf16[2,1,384,1024]{2,3,1,0:T(8,128)(2,1)S(1)}, u32[]{:S(2)}) copy-start(bf16[2,1,384,1024]{2,3,1,0:T(8,128)(2,1)S(1)} %get-tuple-element.31) | copy-start | bytes 4718596
  147.7 8.9 %copy-start.8 = (bf16[2,1,384,1024]{2,3,1,0:T(8,128)(2,1)}, bf16[2,1,384,1024]{2,3,1,0:T(8,128)(2,1)S(1)}, u32[]{:S(2)}) copy-start(bf16[2,1,384,1024]{2,3,1,0:T(8,128)(2,1)S(1)} %get-tuple-element.32) | copy-start | bytes 4718596
  156.6 1.4 copy-start.7
  158.0 13.0 %copy-start.9 = (s32[4,2]{0,1:T(2,128)S(1)}, s32[4,2]{0,1:T(2,128)}, u32[]{:S(2)}) copy-start(s32[4,2]{0,1:T(2,128)} %param.13) | copy-start | bytes 100
  158.0 15.0 %copy-start.10 = (u32[32]{0:T(128)S(1)}, u32[32]{0:T(128)}, u32[]{:S(2)}) copy-start(u32[32]{0:T(128)} %constant.173) | copy-start | bytes 388
  168.1 330.0 %collective-permute-start = (f32[1,2,384,2048]{3,2,1,0:T(8,128)}, f32[1,2,384,2048]{3,2,1,0:T(8,128)}, u32[]{:S(2)}, u32[]{:S(2)}) collective-permute-start(f32[1,2,384,2048]{3,2,1,0:T(8,128)} %convolution_bitcast_fusion), channel_id=1, source_target_pairs={{0,16},{16,0},{1,17},{17,1},{2,18},{18,2},{3,19},{19,3},{4,20},{20... | collective-permute-start | bytes 18874376 | tf_op jit(solution)/shard_map/ppermute | solution.py:13
  493.3 163.3 %all-to-all-start.1 = ((bf16[2,8,64,2048]{3,2,0,1:T(8,128)(2,1)}), bf16[2,8,64,2048]{3,2,0,1:T(8,128)(2,1)}, u32[]{:S(2)}, u32[]{:S(2)}) async-start(bf16[2,8,64,2048]{3,2,0,1:T(8,128)(2,1)} %copy.51), calls=%async_computation.1 | async-start | bytes 8388608 | tf_op jit(solution)/shard_map/all_to_all | solution.py:121
  512.2 3.1 copy-start.3
  512.2 4.2 copy-start.4
  512.2 4.2 copy-start.5
  517.6 62.9 %collective-permute-start.2 = (bf16[1,384,2048]{2,1,0:T(8,128)(2,1)}, bf16[1,384,2048]{2,1,0:T(8,128)(2,1)}, u32[]{:S(2)}, u32[]{:S(2)}) collective-permute-start(bf16[1,384,2048]{2,1,0:T(8,128)(2,1)} %dynamic-slice_bitcast_fusion.2), channel_id=1, source_target_pairs={{0,8},{2,10},{4,12},{6,14},{8,0},{10,2},{12,4},{14,6},{1,9},{3,11}... | collective-permute-start | bytes 4718600 | tf_op jit(solution)/shard_map/ppermute | solution.py:13
  519.6 94.7 %collective-permute-start.1 = (bf16[1,384,2048]{2,1,0:T(8,128)(2,1)}, bf16[1,384,2048]{2,1,0:T(8,128)(2,1)}, u32[]{:S(2)}, u32[]{:S(2)}) collective-permute-start(bf16[1,384,2048]{2,1,0:T(8,128)(2,1)} %dynamic-slice_bitcast_fusion.3), channel_id=1, source_target_pairs={{0,8},{2,10},{4,12},{6,14},{8,0},{10,2},{12,4},{14,6},{1,9},{3,11}... | collective-permute-start | bytes 4718600 | tf_op jit(solution)/shard_map/ppermute | solution.py:13
  519.7 127.8 %collective-permute-start.3 = (bf16[1,384,2048]{2,1,0:T(8,128)(2,1)}, bf16[1,384,2048]{2,1,0:T(8,128)(2,1)}, u32[]{:S(2)}, u32[]{:S(2)}) collective-permute-start(bf16[1,384,2048]{2,1,0:T(8,128)(2,1)} %dynamic-slice_bitcast_fusion.1), channel_id=1, source_target_pairs={{0,8},{2,10},{4,12},{6,14},{8,0},{10,2},{12,4},{14,6},{1,9},{3,11}... | collective-permute-start | bytes 4718600 | tf_op jit(solution)/shard_map/ppermute | solution.py:13
  656.6 4.2 copy-start.1
Sparse Core Ops, SparseCore 0:
  156.7 331.1 all-reduce.2
where the time goes:
time: 669 us; the launch traced here: 668 us
  waiting for transfers between devices  524 us (78%)
  matrix products  52.1 us (8%)
  local copies, waits for them, and re-layouts  39.1 us (6%)
  other arithmetic  19.5 us (3%)
  starting transfers between devices  17.2 us (3%)
  between operations  16.2 us (2%)
    unnamed x2, waiting for transfers between devices  314 us
    ppermute x4, waiting for transfers between devices, partner(): lax.ppermute(value, axis, [(i, i ^ 1 << bit) for i in range(lax.axis_size...  117 us
    all_to_all x1, waiting for transfers between devices, shards(): lax.all_to_all(outgoing, 'expert', split_axis=1, concat_axis=1, tiled=True)  92.4 us
    dot_general x2, matrix products, grad_rows(): jnp.einsum('esd,ecfs->cefd', routed, part_grad, preferred_element_type=jn...  24.1 us
  transfers between devices with their start and end apart: 7, of which 5 were waited for; matrix products, arithmetic and copies ran while one was open for 8% of the time, Pallas kernels for 0%

commit v1 on v0

--- a/solution.py
+++ b/solution.py
@@ -1,6 +1,8 @@
 import jax
 import jax.numpy as jnp
 from jax import lax
+from jax.experimental import pallas as pl
+from jax.experimental.pallas import tpu as pltpu
 from jax.sharding import PartitionSpec as P
 
 beta_one = 0.9
@@ -146,6 +148,367 @@
     return (hidden[None], token_grad, new_weights, new_first, new_second)
 
 
+IDS_COLS = 128
+CORE, X_BIT, Y_BIT = 1, 2, 4
+
+
+def flip(value, axis, mask):
+    return lax.ppermute(value, axis, [(i, i ^ mask) for i in range(lax.axis_size(axis))])
+
+
+def after(value, *others):
+    return lax.optimization_barrier((value, *others))[0]
+
+
+def gather_chips(rows):
+    half = rows.shape[0] // 2
+    low, high = rows[:half], rows[half:]
+    low_y = flip(low, "expert", Y_BIT)
+    high_x = flip(high, "expert", X_BIT)
+    low_x = flip(jnp.concatenate([low, low_y]), "expert", X_BIT)
+    high_y = flip(jnp.concatenate([high, high_x]), "expert", Y_BIT)
+    return jnp.concatenate(
+        [low, high, low_x[:half], high_x, low_y, high_y[:half], low_x[half:], high_y[half:]]
+    )
+
+
+def select_rows(ids, expert, core):
+    rows = ids.shape[0]
+    quarter = rows // 4
+    row = lax.broadcasted_iota(jnp.int32, (rows, rows), 0)
+    col = lax.broadcasted_iota(jnp.int32, (rows, rows), 1)
+    earlier = ((row // quarter == col // quarter) & (col < row)).astype(jnp.bfloat16)
+    hit = jnp.sum(jnp.where(ids == expert.astype(jnp.float32), 1.0, 0.0), axis=1, keepdims=True)
+    hit = jnp.broadcast_to(hit, (rows, rows))
+    rank = jnp.dot(earlier, hit.astype(jnp.bfloat16), preferred_element_type=jnp.float32)
+    part = row // (rows // 2)
+    owner = jnp.where(core == 0, part, 1 - part)
+    base = owner * (rows // 2) + (row % (rows // 2)) // quarter * quarter
+    taken = (rank.astype(jnp.int32) + base == col) & (hit > 0.5)
+    return jnp.where(taken, 1.0, 0.0).astype(jnp.bfloat16)
+
+
+def dot_nt(a, b):
+    return lax.dot_general(a, b, (((1,), (1,)), ((), ())), preferred_element_type=jnp.float32)
+
+
+def dot_tn(a, b):
+    return lax.dot_general(a, b, (((0,), (0,)), ((), ())), preferred_element_type=jnp.float32)
+
+
+def block_rows(a_ref, b_ref, width):
+    rows = jnp.concatenate([a_ref[0], b_ref[0]], axis=0)
+    return rows[:, :width], rows[:, width:].astype(jnp.float32)
+
+
+def gradients(gate, up, grad):
+    sig = jax.nn.sigmoid(gate)
+    grad_gate = grad * up * sig * (1.0 + gate * (1.0 - sig))
+    grad_up = grad * gate * sig
+    return sig, grad_gate, grad_up
+
+
+def own_kernel(info, a_ref, b_ref, w_ref, hg_ref, hidden_ref, grad_ref, ta_ref, tb_ref):
+    core, base, replica = info[1], info[3], info[4]
+    width = w_ref.shape[3]
+    rows, ids = block_rows(a_ref, b_ref, width)
+    half = rows.shape[0] // 2
+    total = None
+    for e in range(w_ref.shape[1]):
+        select = select_rows(ids, base + e, core)
+        gate = dot_nt(w_ref[0, e], rows)
+        up = dot_nt(w_ref[1, e], rows)
+        grad = dot_nt(hg_ref[0, e], select)
+        sig, grad_gate, grad_up = gradients(gate, up, grad)
+        hidden = (gate * sig * up).astype(jnp.bfloat16)
+        hidden_ref[0, e] = jnp.dot(hidden, select, preferred_element_type=jnp.float32).astype(
+            jnp.bfloat16
+        )
+        chosen = jnp.where(replica == 0, grad_gate, grad_up).astype(jnp.bfloat16)
+        grad_ref[e, 0] = chosen[:, :half]
+        grad_ref[e, 1] = chosen[:, half:]
+        term = dot_tn(grad_gate.astype(jnp.bfloat16), w_ref[0, e])
+        term = term + dot_tn(grad_up.astype(jnp.bfloat16), w_ref[1, e])
+        total = term if total is None else total + term
+    total = total.astype(jnp.bfloat16)
+    ta_ref[0] = total[:half]
+    tb_ref[0] = total[half:]
+
+
+def other_kernel(info, a_ref, b_ref, w_ref, hg_ref, grad_ref):
+    expert, core, base, replica = info[0], info[1], info[3], info[4]
+    width = w_ref.shape[3]
+    rows, ids = block_rows(a_ref, b_ref, width)
+    half = rows.shape[0] // 2
+    select = select_rows(ids, base + expert, core)
+    gate = dot_nt(w_ref[0, 0], rows)
+    up = dot_nt(w_ref[1, 0], rows)
+    grad = dot_nt(hg_ref[...], select)
+    _, grad_gate, grad_up = gradients(gate, up, grad)
+    chosen = jnp.where(replica == 0, grad_gate, grad_up).astype(jnp.bfloat16)
+    grad_ref[0] = chosen[:, :half]
+    grad_ref[1] = chosen[:, half:]
+
+
+def weight_gradient(own_ref, other_ref, tokens):
+    a_ref, b_ref, c_ref, d_ref = tokens
+    return (
+        jnp.dot(own_ref[0, 0], a_ref[...], preferred_element_type=jnp.float32)
+        + jnp.dot(own_ref[0, 1], b_ref[...], preferred_element_type=jnp.float32)
+        + jnp.dot(other_ref[0], c_ref[...], preferred_element_type=jnp.float32)
+        + jnp.dot(other_ref[1], d_ref[...], preferred_element_type=jnp.float32)
+    )
+
+
+def moments(grad, first, second):
+    first = beta_one * first.astype(jnp.float32) + (1.0 - beta_one) * grad
+    second = beta_two * second.astype(jnp.float32) + (1.0 - beta_two) * grad * grad
+    return first, second
+
+
+def step_weights(weight, first, second):
+    return weight.astype(jnp.float32) - step_size * first / (jnp.sqrt(second) + adam_eps)
+
+
+def leaving_kernel(info, own, other, a, b, c, d, m_ref, v_ref, first_ref, second_ref):
+    grad = weight_gradient(own, other, (a, b, c, d))
+    first, second = moments(grad, m_ref[0, 0], v_ref[0, 0])
+    first_ref[...] = first.astype(jnp.bfloat16)
+    second_ref[...] = second.astype(jnp.bfloat16)
+
+
+def staying_kernel(info, own, other, a, b, c, d, m_ref, v_ref, w_ref, nw_ref, nm_ref, nv_ref):
+    grad = weight_gradient(own, other, (a, b, c, d))
+    first, second = moments(grad, m_ref[0, 0], v_ref[0, 0])
+    nw_ref[0, 0] = step_weights(w_ref[0, 0], first, second).astype(jnp.bfloat16)
+    nm_ref[0, 0] = first.astype(jnp.bfloat16)
+    nv_ref[0, 0] = second.astype(jnp.bfloat16)
+
+
+def arriving_kernel(info, _w, _m, _v, w_ref, m_ref, v_ref, nw_ref, nm_ref, nv_ref):
+    first, second = m_ref[...], v_ref[...]
+    nw_ref[0, 0] = step_weights(
+        w_ref[...], first.astype(jnp.float32), second.astype(jnp.float32)
+    ).astype(jnp.bfloat16)
+    nm_ref[0, 0] = first
+    nv_ref[0, 0] = second
+
+
+def call(kernel, grid, in_specs, out_specs, out_shape, flops, bytes_accessed, **extra):
+    return pl.pallas_call(
+        kernel,
+        grid_spec=pltpu.PrefetchScalarGridSpec(
+            num_scalar_prefetch=1, grid=grid, in_specs=in_specs, out_specs=out_specs
+        ),
+        out_shape=out_shape,
+        cost_estimate=pl.CostEstimate(
+            flops=flops, bytes_accessed=bytes_accessed, transcendentals=0
+        ),
+        **extra,
+    )
+
+
+def fast_shards(tokens, expert_ids, weights, first_moment, second_moment, hidden_grad, swap_list):
+    owners = lax.axis_size("expert")
+    row_count, width = tokens.shape
+    _, per_dev, hidden_units, slots_total = hidden_grad.shape
+    chips = owners // 2
+    bf16 = jnp.bfloat16
+    replica = lax.axis_index("dp")
+    own_index = lax.axis_index("expert")
+    quarter = lax.axis_index("tensor")
+    chosen, _ = migration_slot(swap_list, per_dev)
+    staying = 1 - chosen
+    core, chip, base = own_index % 2, own_index // 2, own_index * per_dev
+    info_leave = jnp.stack([chosen, core, chip, base, replica]).astype(jnp.int32)
+    info_stay = jnp.stack([staying, core, chip, base, replica]).astype(jnp.int32)
+
+    ids = jnp.pad(
+        expert_ids.astype(bf16), ((0, 0), (0, IDS_COLS - expert_ids.shape[1])), constant_values=-1
+    )
+    rows = jnp.concatenate([tokens, ids], axis=1)
+    own_a = gather_chips(rows)
+    own_b = flip(own_a, "expert", CORE)
+    crossed = flip(rows, "dp", 1)
+    other_a = gather_chips(crossed)
+    other_b = flip(other_a, "expert", CORE)
+
+    leave_grad = lax.dynamic_index_in_dim(hidden_grad[0], chosen, 0, keepdims=False)
+    stay_grad = lax.dynamic_index_in_dim(hidden_grad[0], staying, 0, keepdims=False)
+    leave_other = flip(after(leave_grad, crossed), "dp", 1)
+    stay_other = flip(after(stay_grad, leave_other), "dp", 1)
+
+    weight_half = lax.dynamic_index_in_dim(weights, replica, 0, keepdims=False)
+    leave_weight = lax.dynamic_index_in_dim(weight_half, chosen, 0, keepdims=False)
+    new_weight_in = flip(after(leave_weight, own_a), "expert", Y_BIT)
+
+    wide = rows.shape[1]
+    blocks = lambda value: value.reshape(chips, row_count, wide)
+    token_spec = pl.BlockSpec((1, row_count, wide), lambda k, info: (k, 0, 0))
+    at_chip = lambda k, info: jnp.bitwise_xor(info[2], k)
+    pair = 2 * row_count
+    matmul = 2 * per_dev * hidden_units * width * chips * pair * 2
+    hidden, own_grad, ta, tb = call(
+        own_kernel,
+        (chips,),
+        [
+            token_spec,
+            token_spec,
+            pl.BlockSpec(weights.shape, lambda k, info: (0, 0, 0, 0), pipeline_mode=pl.Buffered(1)),
+            pl.BlockSpec(
+                (1, per_dev, hidden_units, pair), lambda k, info: (0, 0, 0, at_chip(k, info))
+            ),
+        ],
+        [
+            pl.BlockSpec(
+                (1, per_dev, hidden_units, pair), lambda k, info: (0, 0, 0, at_chip(k, info))
+            ),
+            pl.BlockSpec((per_dev, 2, hidden_units, row_count), lambda k, info: (0, 0, 0, k)),
+            pl.BlockSpec((1, row_count, width), lambda k, info: (k, 0, 0)),
+            pl.BlockSpec((1, row_count, width), lambda k, info: (k, 0, 0)),
+        ],
+        [
+            jax.ShapeDtypeStruct(hidden_grad.shape, bf16),
+            jax.ShapeDtypeStruct((per_dev, 2, hidden_units, chips * row_count), bf16),
+            jax.ShapeDtypeStruct((chips, row_count, width), bf16),
+            jax.ShapeDtypeStruct((chips, row_count, width), bf16),
+        ],
+        2 * matmul,
+        20 << 20,
+    )(info_leave, blocks(own_a), blocks(own_b), weights, hidden_grad)
+
+    def other_grad(info, grad):
+        return call(
+            other_kernel,
+            (chips,),
+            [
+                token_spec,
+                token_spec,
+                pl.BlockSpec(
+                    (2, 1, hidden_units, width),
+                    lambda k, info: (0, info[0], 0, 0),
+                    pipeline_mode=pl.Buffered(1),
+                ),
+                pl.BlockSpec((hidden_units, pair), lambda k, info: (0, at_chip(k, info))),
+            ],
+            pl.BlockSpec((2, hidden_units, row_count), lambda k, info: (0, 0, k)),
+            jax.ShapeDtypeStruct((2, hidden_units, chips * row_count), bf16),
+            matmul // 2,
+            9 << 20,
+        )(info, blocks(other_a), blocks(other_b), weights, grad)
+
+    tile = 256
+    tiles = width // tile
+    flat_rows = chips * row_count
+    flat_spec = pl.BlockSpec((flat_rows, tile), lambda j, info: (0, j))
+    state_spec = pl.BlockSpec(
+        (1, 1, hidden_units, tile), lambda j, info: (0, info[0], 0, j)
+    )
+    grad_specs = [
+        pl.BlockSpec((1, 2, hidden_units, flat_rows), lambda j, info: (info[0], 0, 0, 0)),
+        pl.BlockSpec((2, hidden_units, flat_rows), lambda j, info: (0, 0, 0)),
+        flat_spec,
+        flat_spec,
+        flat_spec,
+        flat_spec,
+    ]
+    plain_spec = pl.BlockSpec((hidden_units, tile), lambda j, info: (0, j))
+    plain_shape = jax.ShapeDtypeStruct((hidden_units, width), bf16)
+    leave_first, leave_second = call(
+        leaving_kernel,
+        (tiles,),
+        grad_specs + [state_spec, state_spec],
+        [plain_spec, plain_spec],
+        [plain_shape, plain_shape],
+        matmul // 2,
+        18 << 20,
+    )(
+        info_leave,
+        own_grad,
+        other_grad(info_leave, leave_other),
+        own_a,
+        own_b,
+        other_a,
+        other_b,
+        first_moment,
+        second_moment,
+    )
+    second_in = flip(leave_second, "expert", Y_BIT)
+    first_in = flip(leave_first, "expert", Y_BIT)
+
+    state_shape = jax.ShapeDtypeStruct(first_moment.shape, bf16)
+    stay_states = call(
+        staying_kernel,
+        (tiles,),
+        grad_specs
+        + [
+            state_spec,
+            state_spec,
+            pl.BlockSpec((1, 1, hidden_units, tile), lambda j, info: (info[4], info[0], 0, j)),
+        ],
+        [state_spec] * 3,
+        [state_shape] * 3,
+        matmul // 2,
+        20 << 20,
+    )(
+        info_stay,
+        own_grad,
+        other_grad(info_stay, stay_other),
+        own_a,
+        own_b,
+        other_a,
+        other_b,
+        first_moment,
+        second_moment,
+        weights,
+    )
+
+    f32 = jnp.float32
+    core_sum = ta.astype(f32) + flip(tb, "expert", CORE).astype(f32)
+    core_sum = core_sum.reshape(2, 2, row_count, width)
+    x_sum = core_sum[:, 0] + flip(core_sum[:, 1].astype(bf16), "expert", X_BIT).astype(f32)
+    x_sum = x_sum.reshape(2, 2, row_count // 2, width)
+    mine = lax.dynamic_index_in_dim(x_sum, quarter, 1, keepdims=False)
+    theirs = lax.dynamic_index_in_dim(x_sum, 1 - quarter, 1, keepdims=False)
+    z_sum = mine + flip(theirs.astype(bf16), "tensor", 1).astype(f32)
+    token_grad = z_sum[0] + flip(z_sum[1].astype(bf16), "expert", Y_BIT).astype(f32)
+
+    row_tile = 128
+    any_spec = pl.BlockSpec(memory_space=pl.ANY)
+    in_spec = pl.BlockSpec((row_tile, width), lambda i, info: (i, 0))
+    out_spec = pl.BlockSpec((1, 1, row_tile, width), lambda i, info: (0, info[0], i, 0))
+    new_weights, new_first, new_second = call(
+        arriving_kernel,
+        (hidden_units // row_tile,),
+        [any_spec] * 3 + [in_spec] * 3,
+        [out_spec] * 3,
+        [state_shape] * 3,
+        0,
+        9 << 20,
+        input_output_aliases={1: 0, 2: 1, 3: 2},
+    )(info_leave, *stay_states, new_weight_in, first_in, second_in)
+    return (hidden, token_grad.astype(bf16), new_weights, new_first, new_second)
+
+
+def token_layout_fits(tokens, expert_ids, weights, first, second, hidden_grad, swap_list):
+    owners, parts = lax.axis_size("expert"), lax.axis_size("tensor")
+    return (
+        lax.axis_size("dp") == 2
+        and owners == 8
+        and parts == 2
+        and weights.shape[1] == 2
+        and 2 * swap_list.shape[0] == owners
+        and tokens.shape[0] == 128
+        and hidden_grad.shape[3] == owners * tokens.shape[0]
+        and weights.shape[2] % 128 == 0
+        and tokens.shape[1] % 256 == 0
+    )
+
+
+def plan(*args):
+    return fast_shards(*args) if token_layout_fits(*args) else shards(*args)
+
+
 def solution(mesh):
     in_specs = (
         P(("dp", "expert"), None),
@@ -163,4 +526,4 @@
         P("dp", "expert", "tensor", None),
         P("dp", "expert", "tensor", None),
     )
-    return jax.shard_map(shards, mesh=mesh, in_specs=in_specs, out_specs=out_specs, check_vma=False)
+    return jax.shard_map(plan, mesh=mesh, in_specs=in_specs, out_specs=out_specs, check_vma=False)

time: 669 us -> 227 us (0.34)
  waiting for transfers between devices: 524 us -> 103 us
  Pallas kernels: 0 us -> 71.5 us
  matrix products: 52.1 us -> 0 us
  local copies, waits for them, and re-layouts: 39.1 us -> 15.4 us
  between operations: 16.2 us -> 4.12 us
  other arithmetic: 19.5 us -> 10.6 us
    unnamed x2 -> x0, waiting for transfers between devices: 314 us -> none
    all_to_all x2 -> x0, waiting for transfers between devices: 92.4 us -> none  [the longest x1 92.4 us: shards(): lax.all_to_all(outgoing, 'expert', split_axis=1, concat_axis=1, tiled=True)]
    pallas_call x0 -> x6, Pallas kernels: none -> 71.5 us  [the longest x1 23.7 us: fast_shards(): call(own_kernel, (chips,), [token_spec, token_spec, pl.BlockSpec(weights....]
    dot_general x7 -> x0, matrix products: 52.1 us -> none  [the longest x2 24.1 us: grad_rows(): jnp.einsum('esd,ecfs->cefd', routed, part_grad, preferred_element_type=jn...]
    ppermute x4 -> x20, waiting for transfers between devices: 117 us -> 103 us  [flip(): lax.ppermute(value, axis, [(i, i ^ mask) for i in range(lax.axis_size(axi...]
    ppermute x4 -> x20, starting transfers between devices: 6.95 us -> 21.2 us  [flip(): lax.ppermute(value, axis, [(i, i ^ mask) for i in range(lax.axis_size(axi...]
    reshape x4 -> x0, local copies, waits for them, and re-layouts: 14 us -> none  [the longest x1 8.27 us: shards(): outgoing.reshape(per_dev, owners, tensor_count * capacity, model_width)]
    all_to_all x2 -> x0, local copies, waits for them, and re-layouts: 11 us -> none  [the longest x1 8.42 us: shards(): lax.all_to_all(outgoing, 'expert', split_axis=1, concat_axis=1, tiled=True)]
  transfers between devices with their start and end apart: 7 -> 20, of which waited for: 5 -> 9; matrix products, arithmetic and copies ran while one was open for 8% -> 9% of each run, Pallas kernels for 0% -> 32%
where the time goes in v1:
time: 227 us; the launch traced here: 226 us
  waiting for transfers between devices  103 us (45%)
  Pallas kernels  71.5 us (31%)
  starting transfers between devices  21.2 us (9%)
  local copies, waits for them, and re-layouts  15.4 us (7%)
  other arithmetic  10.6 us (5%)
  between operations  4.12 us (2%)
    ppermute x20, waiting for transfers between devices, flip(): lax.ppermute(value, axis, [(i, i ^ mask) for i in range(lax.axis_size(axi...  103 us
    pallas_call x1, Pallas kernels, fast_shards(): call(own_kernel, (chips,), [token_spec, token_spec, pl.BlockSpec(weights....  23.7 us
    ppermute x20, starting transfers between devices, flip(): lax.ppermute(value, axis, [(i, i ^ mask) for i in range(lax.axis_size(axi...  21.2 us
    pallas_call x2, Pallas kernels, other_grad(): call(other_kernel, (chips,), [token_spec, token_spec, pl.BlockSpec((2, 1,...  17.5 us
    pallas_call x1, Pallas kernels, fast_shards(): call(staying_kernel, (tiles,), grad_specs + [state_spec, state_spec, pl.B...  12.6 us
    pallas_call x1, Pallas kernels, fast_shards(): call(leaving_kernel, (tiles,), grad_specs + [state_spec, state_spec], [pl...  11.1 us
    pallas_call x1, Pallas kernels, fast_shards(): call(arriving_kernel, (hidden_units // row_tile,), [any_spec] * 3 + [in_s...  6.53 us
    unnamed x19, local copies, waits for them, and re-layouts  5.79 us
  transfers between devices with their start and end apart: 20, of which 9 were waited for; matrix products, arithmetic and copies ran while one was open for 9% of the time, Pallas kernels for 32%

profile of v1, /device:TPU:0, one launch (start us, length us, event | category | flops | bytes accessed | tf_op | source)
XLA Modules:
  0.0 225.7 jit_solution(13855314414473968766)
XLA Ops:
  0.6 0.7 convert_element_type.37
  1.5 1.9 fusion.3
  3.4 3.1 %collective-permute-start = (bf16[64,2176]{1,0:T(8,128)(2,1)S(1)}, bf16[64,2176]{1,0:T(8,128)(2,1)S(1)}, u32[]{:S(2)}, u32[]{:S(2)}) collective-permute-start(bf16[64,2176]{1,0:T(8,128)(2,1)S(1)} %get-tuple-element.40), channel_id=1, source_target_pairs={{0,8},{2,10},{4,12},{6,14},{8,0},{10,2},{12,4},{14,6},{1,9},{3,11}... | collective-permute-start | bytes 835592 | tf_op jit(solution)/shard_map/ppermute | solution.py:156
  6.5 2.6 %collective-permute-start.9 = (bf16[128,2176]{1,0:T(8,128)(2,1)S(1)}, bf16[128,2176]{1,0:T(8,128)(2,1)S(1)}, u32[]{:S(2)}, u32[]{:S(2)}) collective-permute-start(bf16[128,2176]{1,0:T(8,128)(2,1)S(1)} %get-tuple-element.41), channel_id=1, source_target_pairs={{0,16},{16,0},{1,17},{17,1},{2,18},{18,2},{3,19},{19,3},{4,20},{20... | collective-permute-start | bytes 1671176 | tf_op jit(solution)/shard_map/ppermute | solution.py:156
  9.1 1.5 collective-permute-start.2
  10.6 0.6 add_reduce_fusion
  11.2 1.3 stack.33.info
  12.5 0.6 collective-permute-done
  13.2 1.8 collective-permute-start.1
  15.0 3.6 %collective-permute-done.2 = bf16[64,2176]{1,0:T(8,128)(2,1)S(1)} collective-permute-done((bf16[64,2176]{1,0:T(8,128)(2,1)S(1)}, bf16[64,2176]{1,0:T(8,128)(2,1)S(1)}, u32[]{:S(2)}, u32[]{:S(2)}) %collective-permute-start.2) | collective-permute-done | bytes 278560 | tf_op jit(solution)/shard_map/ppermute | solution.py:156
  18.7 14.7 %collective-permute-done.9 = bf16[128,2176]{1,0:T(8,128)(2,1)S(1)} collective-permute-done((bf16[128,2176]{1,0:T(8,128)(2,1)S(1)}, bf16[128,2176]{1,0:T(8,128)(2,1)S(1)}, u32[]{:S(2)}, u32[]{:S(2)}) %collective-permute-start.9) | collective-permute-done | bytes 557088 | tf_op jit(solution)/shard_map/ppermute | solution.py:156
  33.5 0.5 collective-permute-start.10
  34.0 1.5 collective-permute-start.12
  35.5 0.7 slice_dynamic-update-slice_fusion.7
  36.3 0.7 constant_dynamic-update-slice_fusion.1
  37.0 0.7 constant_dynamic-update-slice_fusion
  37.7 0.7 slice_dynamic-update-slice_fusion.6
  38.5 0.7 slice_dynamic-update-slice_fusion.5
  39.2 0.7 slice_dynamic-update-slice_fusion.4.a
  39.9 1.2 collective-permute-done.10
  41.1 1.6 collective-permute-start.11
  42.8 0.8 pad_maximum_fusion.3
  44.1 11.0 %collective-permute-done.11 = bf16[128,2176]{1,0:T(8,128)(2,1)S(1)} collective-permute-done((bf16[128,2176]{1,0:T(8,128)(2,1)S(1)}, bf16[128,2176]{1,0:T(8,128)(2,1)S(1)}, u32[]{:S(2)}, u32[]{:S(2)}) %collective-permute-start.11) | collective-permute-done | bytes 557088 | tf_op jit(solution)/shard_map/ppermute | solution.py:156
  55.2 23.7 %shard_map.110 = (bf16[1,2,384,1024]{3,2,1,0:T(8,128)(2,1)}, bf16[2,2,384,512]{3,2,1,0:T(8,128)(2,1)}, bf16[4,128,2048]{2,1,0:T(8,128)(2,1)}, bf16[4,128,2048]{2,1,0:T(8,128)(2,1)}) custom-call(s32[5]{0:T(128)} %stack.33.info, bf16[4,128,2176]{2,1,0:T(8,128)(2,1)} %bitcast.7.a_ref, bf16[4,128,2176]{2,1,0:T(8,128)(2,1)} %bitcast.8.b_ref, ...), custom_call_target="tpu_custom_call" | custom-call | flops 12884901888 | bytes 20971520 | tf_op jit(solution)/shard_map/pallas_call | solution.py:351
  79.0 0.6 collective-permute-start.14
  82.9 2.8 %dynamic-slice_bitcast_fusion.1 = (bf16[384,1024]{1,0:T(8,128)(2,1)}, bf16[384,1024]{1,0:T(8,128)(2,1)}) fusion(bf16[1,2,384,1024]{3,2,1,0:T(8,128)(2,1)} %hg_ref.1, s32[]{:T(128)S(6)} %select_n.71, s32[]{:T(128)S(6)} %select_n.70), kind=kLoop, calls=%fused_computation.10 | loop fusion | bytes 3145736 | tf_op jit(solution)/shard_map/jit(dynamic_index_in_dim)/squeeze | solution.py:336
  85.7 2.3 %convert_add_fusion = f32[4,128,2048]{2,1,0:T(8,128)S(1)} fusion(bf16[4,128,2048]{2,1,0:T(8,128)(2,1)} %collective-permute-done.5, bf16[4,128,2048]{2,1,0:T(8,128)(2,1)S(1)} %copy-done.2), kind=kLoop, calls=%fused_computation | loop fusion | flops 3145728 | bytes 8388608 | tf_op jit(solution)/shard_map/add | solution.py:467
  88.1 1.9 copy-done.1
  90.0 1.1 fusion.2
  91.6 2.8 %dynamic-slice_bitcast_fusion = bf16[384,2048]{1,0:T(8,128)(2,1)} fusion(bf16[2,2,384,2048]{3,2,1,0:T(8,128)(2,1)} %w_ref.7, s32[]{:T(128)S(6)} %select_n.73, s32[]{:T(128)S(6)} %select_n.74), kind=kLoop, calls=%fused_computation.4 | loop fusion | bytes 3145736 | tf_op jit(solution)/shard_map/jit(dynamic_index_in_dim)/squeeze | solution.py:342
  94.4 1.6 collective-permute-start.17
  95.9 27.3 %collective-permute-done.15.hg_ref = bf16[384,1024]{1,0:T(8,128)(2,1)} collective-permute-done((bf16[384,1024]{1,0:T(8,128)(2,1)}, bf16[384,1024]{1,0:T(8,128)(2,1)}, u32[]{:S(2)}, u32[]{:S(2)}) %collective-permute-start.15) | collective-permute-done | bytes 786464 | tf_op jit(solution)/shard_map/ppermute | solution.py:156
  123.2 8.7 %shard_map.113.other = bf16[2,384,512]{2,1,0:T(8,128)(2,1)} custom-call(s32[5]{0:T(128)} %stack.33.info, bf16[4,128,2176]{2,1,0:T(8,128)(2,1)} %bitcast.56, bf16[4,128,2176]{2,1,0:T(8,128)(2,1)} %bitcast.19.b_ref, bf16[2,2,384,2048]{3,2,1,0:T(8,128)(2,1)} %w_ref.7, bf16[384,1024]{1,0:T(8,128)(2,1)} %collective-permute-done.15.hg_ref), custom_call_target="tpu_custom_call" | custom-call | flops 3221225472 | bytes 9437184 | tf_op jit(solution)/shard_map/pallas_call | solution.py:381
  132.0 2.2 fusion
  134.2 1.8 collective-permute-start.7
  136.0 11.1 %shard_map.114 = (bf16[384,2048]{1,0:T(8,128)(2,1)}, bf16[384,2048]{1,0:T(8,128)(2,1)}) custom-call(s32[5]{0:T(128)} %stack.33.info, bf16[2,2,384,512]{3,2,1,0:T(8,128)(2,1)} %get-tuple-element.23.own, bf16[2,384,512]{2,1,0:T(8,128)(2,1)} %shard_map.113.other, bf16[512,2176]{1,0:T(8,128)(2,1)} %slice_dynamic-update-slice_fusion.4.a, ...), custom_call_target="tpu_custom_call" | custom-call | flops 3221225472 | bytes 18874368 | tf_op jit(solution)/shard_map/pallas_call | solution.py:417
  147.1 1.6 collective-permute-start.18
  148.7 0.5 collective-permute-start.19
  149.2 0.6 stack.35.info
  149.8 9.6 %collective-permute-done.16.hg_ref = bf16[384,1024]{1,0:T(8,128)(2,1)} collective-permute-done((bf16[384,1024]{1,0:T(8,128)(2,1)}, bf16[384,1024]{1,0:T(8,128)(2,1)}, u32[]{:S(2)}, u32[]{:S(2)}) %collective-permute-start.16) | collective-permute-done | bytes 786464 | tf_op jit(solution)/shard_map/ppermute | solution.py:156
  159.4 8.8 %shard_map.111.other = bf16[2,384,512]{2,1,0:T(8,128)(2,1)} custom-call(s32[5]{0:T(128)} %stack.35.info, bf16[4,128,2176]{2,1,0:T(8,128)(2,1)} %bitcast.57, bf16[4,128,2176]{2,1,0:T(8,128)(2,1)} %bitcast.19.b_ref, bf16[2,2,384,2048]{3,2,1,0:T(8,128)(2,1)} %w_ref.7, bf16[384,1024]{1,0:T(8,128)(2,1)} %collective-permute-done.16.hg_ref), custom_call_target="tpu_custom_call" | custom-call | flops 3221225472 | bytes 9437184 | tf_op jit(solution)/shard_map/pallas_call | solution.py:381
  168.2 1.1 bitcast_add_fusion
  169.4 1.6 collective-permute-start.8
  170.9 12.6 %shard_map.112 = (bf16[1,2,384,2048]{3,2,1,0:T(8,128)(2,1)}, bf16[1,2,384,2048]{3,2,1,0:T(8,128)(2,1)}, bf16[1,2,384,2048]{3,2,1,0:T(8,128)(2,1)}) custom-call(s32[5]{0:T(128)} %stack.35.info, bf16[2,2,384,512]{3,2,1,0:T(8,128)(2,1)} %get-tuple-element.23.own, bf16[2,384,512]{2,1,0:T(8,128)(2,1)} %shard_map.111.other, ...), custom_call_target="tpu_custom_call" | custom-call | flops 3221225472 | bytes 20971520 | tf_op jit(solution)/shard_map/pallas_call | solution.py:440
  183.5 1.2 collective-permute-done.18.m_ref
  184.7 33.7 %collective-permute-done.19.v_ref = bf16[384,2048]{1,0:T(8,128)(2,1)} collective-permute-done((bf16[384,2048]{1,0:T(8,128)(2,1)}, bf16[384,2048]{1,0:T(8,128)(2,1)}, u32[]{:S(2)}, u32[]{:S(2)}) %collective-permute-start.19) | collective-permute-done | bytes 1572896 | tf_op jit(solution)/shard_map/ppermute | solution.py:156
  218.4 6.5 %shard_map.115 = (bf16[1,2,384,2048]{3,2,1,0:T(8,128)(2,1)}, bf16[1,2,384,2048]{3,2,1,0:T(8,128)(2,1)}, bf16[1,2,384,2048]{3,2,1,0:T(8,128)(2,1)}) custom-call(s32[5]{0:T(128)} %stack.33.info, bf16[1,2,384,2048]{3,2,1,0:T(8,128)(2,1)} %get-tuple-element.26._w, ...), custom_call_target="tpu_custom_call", output_to_operand_aliasing={{0}: (1, {}), {1}: (2, {}), {2}: (3, {})} | custom-call | bytes 9437184 | tf_op jit(solution)/shard_map/pallas_call | solution.py:480
  225.0 0.8 fusion.6
  (40 shorter events, 1.7 us)
Async XLA Ops:
  0.6 10.0 %copy-start.3 = (s32[4,2]{0,1:T(2,128)S(1)}, s32[4,2]{0,1:T(2,128)}, u32[]{:S(2)}) copy-start(s32[4,2]{0,1:T(2,128)} %param.13) | copy-start | bytes 100
  3.4 9.7 %collective-permute-start = (bf16[64,2176]{1,0:T(8,128)(2,1)S(1)}, bf16[64,2176]{1,0:T(8,128)(2,1)S(1)}, u32[]{:S(2)}, u32[]{:S(2)}) collective-permute-start(bf16[64,2176]{1,0:T(8,128)(2,1)S(1)} %get-tuple-element.40), channel_id=1, source_target_pairs={{0,8},{2,10},{4,12},{6,14},{8,0},{10,2},{12,4},{14,6},{1,9},{3,11}... | collective-permute-start | bytes 835592 | tf_op jit(solution)/shard_map/ppermute | solution.py:156
  6.5 26.9 %collective-permute-start.9 = (bf16[128,2176]{1,0:T(8,128)(2,1)S(1)}, bf16[128,2176]{1,0:T(8,128)(2,1)S(1)}, u32[]{:S(2)}, u32[]{:S(2)}) collective-permute-start(bf16[128,2176]{1,0:T(8,128)(2,1)S(1)} %get-tuple-element.41), channel_id=1, source_target_pairs={{0,16},{16,0},{1,17},{17,1},{2,18},{18,2},{3,19},{19,3},{4,20},{20... | collective-permute-start | bytes 1671176 | tf_op jit(solution)/shard_map/ppermute | solution.py:156
  9.1 9.5 %collective-permute-start.2 = (bf16[64,2176]{1,0:T(8,128)(2,1)S(1)}, bf16[64,2176]{1,0:T(8,128)(2,1)S(1)}, u32[]{:S(2)}, u32[]{:S(2)}) collective-permute-start(bf16[64,2176]{1,0:T(8,128)(2,1)S(1)} %get-tuple-element.39), channel_id=1, source_target_pairs={{0,4},{2,6},{4,0},{6,2},{8,12},{10,14},{12,8},{14,10},{1,5},{3,7},... | collective-permute-start | bytes 835592 | tf_op jit(solution)/shard_map/ppermute | solution.py:156
  13.2 22.3 %collective-permute-start.1 = (bf16[128,2176]{1,0:T(8,128)(2,1)S(1)}, bf16[128,2176]{1,0:T(8,128)(2,1)S(1)}, u32[]{:S(2)}, u32[]{:S(2)}) collective-permute-start(bf16[128,2176]{1,0:T(8,128)(2,1)S(1)} %pad_maximum_fusion), channel_id=1, source_target_pairs={{0,4},{2,6},{4,0},{6,2},{8,12},{10,14},{12,8},{14,10},{1,5},{3,7},... | collective-permute-start | bytes 1671176 | tf_op jit(solution)/shard_map/ppermute | solution.py:156
  18.7 19.0 %collective-permute-start.3 = (bf16[128,2176]{1,0:T(8,128)(2,1)S(1)}, bf16[128,2176]{1,0:T(8,128)(2,1)S(1)}, u32[]{:S(2)}, u32[]{:S(2)}) collective-permute-start(bf16[128,2176]{1,0:T(8,128)(2,1)S(1)} %pad_maximum_fusion.1), channel_id=1, source_target_pairs={{0,8},{2,10},{4,12},{6,14},{8,0},{10,2},{12,4},{14,6},{1,9},{3,11}... | collective-permute-start | bytes 1671176 | tf_op jit(solution)/shard_map/ppermute | solution.py:156
  33.5 7.6 %collective-permute-start.10 = (bf16[64,2176]{1,0:T(8,128)(2,1)S(1)}, bf16[64,2176]{1,0:T(8,128)(2,1)S(1)}, u32[]{:S(2)}, u32[]{:S(2)}) collective-permute-start(bf16[64,2176]{1,0:T(8,128)(2,1)S(1)} %get-tuple-element.38), channel_id=1, source_target_pairs={{0,8},{2,10},{4,12},{6,14},{8,0},{10,2},{12,4},{14,6},{1,9},{3,11}... | collective-permute-start | bytes 835592 | tf_op jit(solution)/shard_map/ppermute | solution.py:156
  34.0 8.8 %collective-permute-start.12 = (bf16[64,2176]{1,0:T(8,128)(2,1)S(1)}, bf16[64,2176]{1,0:T(8,128)(2,1)S(1)}, u32[]{:S(2)}, u32[]{:S(2)}) collective-permute-start(bf16[64,2176]{1,0:T(8,128)(2,1)S(1)} %get-tuple-element.37), channel_id=1, source_target_pairs={{0,4},{2,6},{4,0},{6,2},{8,12},{10,14},{12,8},{14,10},{1,5},{3,7},... | collective-permute-start | bytes 835592 | tf_op jit(solution)/shard_map/ppermute | solution.py:156
  39.9 15.3 %collective-permute-start.4 = (bf16[512,2176]{1,0:T(8,128)(2,1)}, bf16[512,2176]{1,0:T(8,128)(2,1)}, u32[]{:S(2)}, u32[]{:S(2)}) collective-permute-start(bf16[512,2176]{1,0:T(8,128)(2,1)} %slice_dynamic-update-slice_fusion.4.a), channel_id=1, source_target_pairs={{0,2},{2,0},{4,6},{6,4},{8,10},{10,8},{12,14},{14,12},{1,3},{3,1},... | collective-permute-start | bytes 6684680 | tf_op jit(solution)/shard_map/ppermute | solution.py:156
  41.1 13.9 %collective-permute-start.11 = (bf16[128,2176]{1,0:T(8,128)(2,1)S(1)}, bf16[128,2176]{1,0:T(8,128)(2,1)S(1)}, u32[]{:S(2)}, u32[]{:S(2)}) collective-permute-start(bf16[128,2176]{1,0:T(8,128)(2,1)S(1)} %pad_maximum_fusion.2), channel_id=1, source_target_pairs={{0,4},{2,6},{4,0},{6,2},{8,12},{10,14},{12,8},{14,10},{1,5},{3,7},... | collective-permute-start | bytes 1671176 | tf_op jit(solution)/shard_map/ppermute | solution.py:156
  43.6 35.3 %collective-permute-start.13 = (bf16[128,2176]{1,0:T(8,128)(2,1)}, bf16[128,2176]{1,0:T(8,128)(2,1)S(1)}, u32[]{:S(2)}, u32[]{:S(2)}) collective-permute-start(bf16[128,2176]{1,0:T(8,128)(2,1)} %pad_maximum_fusion.3), channel_id=1, source_target_pairs={{0,8},{2,10},{4,12},{6,14},{8,0},{10,2},{12,4},{14,6},{1,9},{3,11}... | collective-permute-start | bytes 1671176 | tf_op jit(solution)/shard_map/ppermute | solution.py:156
  78.9 6.8 %collective-permute-start.5 = (bf16[4,128,2048]{2,1,0:T(8,128)(2,1)}, bf16[4,128,2048]{2,1,0:T(8,128)(2,1)}, u32[]{:S(2)}, u32[]{:S(2)}) collective-permute-start(bf16[4,128,2048]{2,1,0:T(8,128)(2,1)} %get-tuple-element.22), channel_id=1, source_target_pairs={{0,2},{2,0},{4,6},{6,4},{8,10},{10,8},{12,14},{14,12},{1,3},{3,1},... | collective-permute-start | bytes 6291464 | tf_op jit(solution)/shard_map/ppermute | solution.py:156
  79.0 9.0 %copy-start = (bf16[512,2176]{1,0:T(8,128)(2,1)}, bf16[512,2176]{1,0:T(8,128)(2,1)S(1)}, u32[]{:S(2)}) copy-start(bf16[512,2176]{1,0:T(8,128)(2,1)S(1)} %slice_dynamic-update-slice_fusion.c) | copy-start | bytes 6684676
  79.0 44.2 %collective-permute-start.14 = (bf16[512,2176]{1,0:T(8,128)(2,1)S(1)}, bf16[512,2176]{1,0:T(8,128)(2,1)}, u32[]{:S(2)}, u32[]{:S(2)}) collective-permute-start(bf16[512,2176]{1,0:T(8,128)(2,1)S(1)} %slice_dynamic-update-slice_fusion.c), channel_id=1, source_target_pairs={{0,2},{2,0},{4,6},{6,4},{8,10},{10,8},{12,14},{14,12},{1,3},{3,1},... | collective-permute-start | bytes 6684680 | tf_op jit(solution)/shard_map/ppermute | solution.py:156
  82.9 2.8 %copy-start.2 = (bf16[4,128,2048]{2,1,0:T(8,128)(2,1)S(1)}, bf16[4,128,2048]{2,1,0:T(8,128)(2,1)}, u32[]{:S(2)}) copy-start(bf16[4,128,2048]{2,1,0:T(8,128)(2,1)} %get-tuple-element.21) | copy-start | bytes 6291460
  85.7 37.5 %collective-permute-start.15 = (bf16[384,1024]{1,0:T(8,128)(2,1)}, bf16[384,1024]{1,0:T(8,128)(2,1)}, u32[]{:S(2)}, u32[]{:S(2)}) collective-permute-start(bf16[384,1024]{1,0:T(8,128)(2,1)} %get-tuple-element.24), channel_id=1, source_target_pairs={{0,16},{16,0},{1,17},{17,1},{2,18},{18,2},{3,19},{19,3},{4,20},{20... | collective-permute-start | bytes 2359304 | tf_op jit(solution)/shard_map/ppermute | solution.py:156
  88.0 2.0 copy-start.1
  91.1 40.8 %collective-permute-start.6 = (bf16[2,128,2048]{2,1,0:T(8,128)(2,1)}, bf16[2,128,2048]{2,1,0:T(8,128)(2,1)}, u32[]{:S(2)}, u32[]{:S(2)}) collective-permute-start(bf16[2,128,2048]{2,1,0:T(8,128)(2,1)} %fusion.2), channel_id=1, source_target_pairs={{0,4},{2,6},{4,0},{6,2},{8,12},{10,14},{12,8},{14,10},{1,5},{3,7},... | collective-permute-start | bytes 3145736 | tf_op jit(solution)/shard_map/ppermute | solution.py:156
  94.4 89.2 %collective-permute-start.17 = (bf16[384,2048]{1,0:T(8,128)(2,1)}, bf16[384,2048]{1,0:T(8,128)(2,1)}, u32[]{:S(2)}, u32[]{:S(2)}) collective-permute-start(bf16[384,2048]{1,0:T(8,128)(2,1)} %dynamic-slice_bitcast_fusion), channel_id=1, source_target_pairs={{0,8},{2,10},{4,12},{6,14},{8,0},{10,2},{12,4},{14,6},{1,9},{3,11}... | collective-permute-start | bytes 4718600 | tf_op jit(solution)/shard_map/ppermute | solution.py:156
  123.2 36.2 %collective-permute-start.16 = (bf16[384,1024]{1,0:T(8,128)(2,1)}, bf16[384,1024]{1,0:T(8,128)(2,1)}, u32[]{:S(2)}, u32[]{:S(2)}) collective-permute-start(bf16[384,1024]{1,0:T(8,128)(2,1)} %get-tuple-element.25), channel_id=1, source_target_pairs={{0,16},{16,0},{1,17},{17,1},{2,18},{18,2},{3,19},{19,3},{4,20},{20... | collective-permute-start | bytes 2359304 | tf_op jit(solution)/shard_map/ppermute | solution.py:156
  134.2 34.0 %collective-permute-start.7 = (bf16[2,64,2048]{2,1,0:T(8,128)(2,1)S(1)}, bf16[2,64,2048]{2,1,0:T(8,128)(2,1)}, u32[]{:S(2)}, u32[]{:S(2)}) collective-permute-start(bf16[2,64,2048]{2,1,0:T(8,128)(2,1)S(1)} %fusion.4), channel_id=1, source_target_pairs={{0,1},{1,0},{2,3},{3,2},{4,5},{5,4},{6,7},{7,6},{8,9},{9,8},{10,11... | collective-permute-start | bytes 1572872 | tf_op jit(solution)/shard_map/ppermute | solution.py:156
  147.1 37.6 %collective-permute-start.18 = (bf16[384,2048]{1,0:T(8,128)(2,1)}, bf16[384,2048]{1,0:T(8,128)(2,1)}, u32[]{:S(2)}, u32[]{:S(2)}) collective-permute-start(bf16[384,2048]{1,0:T(8,128)(2,1)} %get-tuple-element.30), channel_id=1, source_target_pairs={{0,8},{2,10},{4,12},{6,14},{8,0},{10,2},{12,4},{14,6},{1,9},{3,11}... | collective-permute-start | bytes 4718600 | tf_op jit(solution)/shard_map/ppermute | solution.py:156
  148.7 69.8 %collective-permute-start.19 = (bf16[384,2048]{1,0:T(8,128)(2,1)}, bf16[384,2048]{1,0:T(8,128)(2,1)}, u32[]{:S(2)}, u32[]{:S(2)}) collective-permute-start(bf16[384,2048]{1,0:T(8,128)(2,1)} %get-tuple-element.31), channel_id=1, source_target_pairs={{0,8},{2,10},{4,12},{6,14},{8,0},{10,2},{12,4},{14,6},{1,9},{3,11}... | collective-permute-start | bytes 4718600 | tf_op jit(solution)/shard_map/ppermute | solution.py:156
  169.4 55.6 %collective-permute-start.8 = (bf16[64,2048]{1,0:T(8,128)(2,1)S(1)}, bf16[64,2048]{1,0:T(8,128)(2,1)S(1)}, u32[]{:S(2)}, u32[]{:S(2)}) collective-permute-start(bf16[64,2048]{1,0:T(8,128)(2,1)S(1)} %fusion.7), channel_id=1, source_target_pairs={{0,8},{2,10},{4,12},{6,14},{8,0},{10,2},{12,4},{14,6},{1,9},{3,11}... | collective-permute-start | bytes 786440 | tf_op jit(solution)/shard_map/ppermute | solution.py:156

commit v2 on v0

--- a/solution.py
+++ b/solution.py
@@ -1,7 +1,10 @@
 import jax
 import jax.numpy as jnp
 from jax import lax
+from jax.experimental import pallas as pl
+from jax.experimental.pallas import tpu as pltpu
 from jax.sharding import PartitionSpec as P
+
 
 beta_one = 0.9
 beta_two = 0.95
@@ -146,21 +149,504 @@
     return (hidden[None], token_grad, new_weights, new_first, new_second)
 
 
+IDS_COLS = 128
+VMEM_GRANT = 26 << 20
+STAY_GRANT = 48 << 20
+CORE, X_BIT, Y_BIT = 1, 2, 4
+DP, EXPERT, TENSOR = "dp", "expert", "tensor"
+
+
+def flip(value, axis, mask):
+    return lax.ppermute(value, axis, [(i, i ^ mask) for i in range(lax.axis_size(axis))])
+
+
+def after(value, *others):
+    return lax.optimization_barrier((value, *others))[0]
+
+
+def gather_chips(rows, direct=False, early=()):
+    by_y = flip(rows, EXPERT, Y_BIT)
+    by_x = flip(rows, EXPERT, X_BIT)
+    if direct:
+        by_xy = flip(rows, EXPERT, X_BIT | Y_BIT)
+    else:
+        by_xy = flip(after(by_y, *early), EXPERT, X_BIT)
+    return [rows, by_x, by_y, by_xy]
+
+
+def gather_plane(columns):
+    result = []
+    for k in range(len(columns[0])):
+        mine = [chips[k] for chips in columns]
+        result.append(mine + [flip(p, EXPERT, CORE) for p in mine])
+    return result
+
+
+def select_rows(ids, expert, core, turned):
+    rows = ids.shape[0]
+    shift = (rows // 4).bit_length() - 1
+    row = lax.broadcasted_iota(jnp.int32, (rows, rows), 0)
+    col = lax.broadcasted_iota(jnp.int32, (rows, rows), 1)
+    quarter = row >> shift
+    earlier = jnp.where((quarter == (col >> shift)) & (col < row), 1.0, 0.0).astype(jnp.bfloat16)
+    hit = jnp.sum(jnp.where(ids == expert.astype(jnp.float32), 1.0, 0.0), axis=1, keepdims=True)
+    hit = jnp.broadcast_to(hit, (rows, rows))
+    rank = jnp.dot(earlier, hit.astype(jnp.bfloat16), preferred_element_type=jnp.float32)
+    base = (quarter ^ (core * 2 + turned)) << shift
+    taken = (rank.astype(jnp.int32) + base == col) & (hit > 0.5)
+    return jnp.where(taken, 1.0, 0.0).astype(jnp.bfloat16)
+
+
+def dot_nt(a, b):
+    return lax.dot_general(a, b, (((1,), (1,)), ((), ())), preferred_element_type=jnp.float32)
+
+
+def dot_tn(a, b):
+    return lax.dot_general(a, b, (((0,), (0,)), ((), ())), preferred_element_type=jnp.float32)
+
+
+def split_rows(rows, width):
+    return rows[:, :width], rows[:, width:].astype(jnp.float32)
+
+
+def take_pieces(pieces, buffer, sems):
+    k, steps = pl.program_id(0), len(pieces)
+
+    def copies(chip, slot):
+        result, start = [], 0
+        for i, piece in enumerate(pieces[chip]):
+            where = buffer.at[slot, pl.ds(start, piece.shape[0])]
+            result.append(pltpu.make_async_copy(piece, where, sems.at[slot, i]))
+            start += piece.shape[0]
+        return result
+
+    for j in range(steps):
+
+        @pl.when(k == j)
+        def _(j=j):
+            if j == 0:
+                for copy in copies(0, 0):
+                    copy.start()
+            if j + 1 < steps:
+                for copy in copies(j + 1, (j + 1) % 2):
+                    copy.start()
+            for copy in copies(j, j % 2):
+                copy.wait()
+
+    return buffer[k % 2]
+
+
+def gradients(gate, up, grad):
+    sig = jax.nn.sigmoid(gate)
+    grad_gate = grad * up * sig * (1.0 + gate * (1.0 - sig))
+    grad_up = grad * gate * sig
+    return sig, grad_gate, grad_up
+
+
+def own_kernel(pieces, info, w_ref, hg_ref, hidden_ref, grad_ref, rows_ref, buffer, sems):
+    core, base = info[2], info[4]
+    width = w_ref.shape[3]
+    rows_ref[...] = take_pieces(pieces, buffer, sems)
+    rows, ids = split_rows(rows_ref[...], width)
+    per_dev, units = w_ref.shape[1], w_ref.shape[2]
+    projected = dot_nt(w_ref[...].reshape(2 * per_dev * units, width), rows)
+    projected = projected.reshape(2, per_dev, units, rows.shape[0])
+    for e in range(per_dev):
+        select = select_rows(ids, base + e, core, 0)
+        gate, up = projected[0, e], projected[1, e]
+        grad = dot_nt(hg_ref[0, e], select)
+        sig, grad_gate, grad_up = gradients(gate, up, grad)
+        hidden = (gate * sig * up).astype(jnp.bfloat16)
+        hidden_ref[0, e] = jnp.dot(hidden, select, preferred_element_type=jnp.float32).astype(
+            jnp.bfloat16
+        )
+        grad_ref[0, e] = grad_gate.astype(jnp.bfloat16)
+        grad_ref[1, e] = grad_up.astype(jnp.bfloat16)
+
+
+def token_kernel(info, grad_ref, w_ref, ta_ref, tb_ref):
+    grad, weight = grad_ref[...], w_ref[...]
+    grad = grad.reshape(-1, grad.shape[-1])
+    total = dot_tn(grad, weight.reshape(-1, weight.shape[-1])).astype(jnp.bfloat16)
+    half = ta_ref.shape[0]
+    ta_ref[...] = total[:half]
+    tb_ref[...] = total[half:]
+
+
+def other_gradient(slot, info, rows, w_ref, hg_ref):
+    expert, core, base, replica = info[slot], info[2], info[4], info[5]
+    units, width = w_ref.shape[2:]
+    rows, ids = split_rows(rows, width)
+    select = select_rows(ids, base + expert, core, info[6])
+    projected = dot_nt(w_ref[...].reshape(2 * units, width), rows)
+    gate, up = projected[:units], projected[units:]
+    grad = dot_nt(hg_ref[...], select)
+    _, grad_gate, grad_up = gradients(gate, up, grad)
+    return jnp.where(replica == 0, grad_gate, grad_up).astype(jnp.bfloat16)
+
+
+def first_other_kernel(slot, pieces, info, w_ref, hg_ref, grad_ref, rows_ref, buffer, sems):
+    rows_ref[...] = take_pieces(pieces, buffer, sems)
+    grad_ref[...] = other_gradient(slot, info, rows_ref[...], w_ref, hg_ref)
+
+
+def other_kernel(slot, info, rows_ref, w_ref, hg_ref, grad_ref):
+    grad_ref[...] = other_gradient(slot, info, rows_ref[...], w_ref, hg_ref)
+
+
+def weight_gradient(own_ref, other_ref, own_rows, other_rows):
+    return jnp.dot(
+        own_ref[0, 0], own_rows[...], preferred_element_type=jnp.float32
+    ) + jnp.dot(other_ref[...], other_rows[...], preferred_element_type=jnp.float32)
+
+
+def moments(grad, first, second):
+    first = beta_one * first.astype(jnp.float32) + (1.0 - beta_one) * grad
+    second = beta_two * second.astype(jnp.float32) + (1.0 - beta_two) * grad * grad
+    return first, second
+
+
+def step_weights(weight, first, second):
+    return weight.astype(jnp.float32) - step_size * first / (jnp.sqrt(second) + adam_eps)
+
+
+def leaving_kernel(info, own, other, a, b, m_ref, v_ref, *out_refs):
+    grad = weight_gradient(own, other, a, b)
+    first, second = moments(grad, m_ref[0, 0], v_ref[0, 0])
+    start = 0
+    for first_ref, second_ref in zip(out_refs[0::2], out_refs[1::2]):
+        stop = start + first_ref.shape[0]
+        first_ref[...] = first[start:stop].astype(jnp.bfloat16)
+        second_ref[...] = second[start:stop].astype(jnp.bfloat16)
+        start = stop
+
+
+def staying_kernel(info, own, other, a, b, m_ref, v_ref, w_ref, nw_ref, nm_ref, nv_ref):
+    grad = weight_gradient(own, other, a, b)
+    first, second = moments(grad, m_ref[0, 0], v_ref[0, 0])
+    nw_ref[0, 0] = step_weights(w_ref[0, 0], first, second).astype(jnp.bfloat16)
+    nm_ref[0, 0] = first.astype(jnp.bfloat16)
+    nv_ref[0, 0] = second.astype(jnp.bfloat16)
+
+
+def arriving_kernel(info, _w, _m, _v, w_ref, m_ref, v_ref, nw_ref, nm_ref, nv_ref):
+    height, span = 16, 1024
+    for start in range(0, w_ref.shape[0], height):
+        for left in range(0, w_ref.shape[1], span):
+            at = (pl.ds(start, height), pl.ds(left, span))
+            first, second = m_ref[at], v_ref[at]
+            nw_ref[(0, 0, *at)] = step_weights(
+                w_ref[at], first.astype(jnp.float32), second.astype(jnp.float32)
+            ).astype(jnp.bfloat16)
+            nm_ref[(0, 0, *at)] = first
+            nv_ref[(0, 0, *at)] = second
+
+
+def call(
+    kernel,
+    grid,
+    in_specs,
+    out_specs,
+    out_shape,
+    flops,
+    moved,
+    scratch=(),
+    grant=VMEM_GRANT,
+    **extra,
+):
+    def run(*args):
+        return pl.pallas_call(
+            kernel,
+            grid_spec=pltpu.PrefetchScalarGridSpec(
+                num_scalar_prefetch=1,
+                grid=grid,
+                in_specs=in_specs,
+                out_specs=out_specs,
+                scratch_shapes=scratch,
+            ),
+            out_shape=out_shape,
+            compiler_params=pltpu.CompilerParams(vmem_limit_bytes=grant),
+            cost_estimate=pl.CostEstimate(
+                flops=flops, bytes_accessed=moved, transcendentals=0
+            ),
+            **extra,
+        )(*args)
+
+    return run
+
+
+LEAVE, STAY = 0, 1
+
+
+def fast_shards(tokens, expert_ids, weights, first_moment, second_moment, hidden_grad, swap_list):
+    owners = lax.axis_size(EXPERT)
+    row_count, width = tokens.shape
+    _, per_dev, hidden_units, _ = hidden_grad.shape
+    chips = owners // 2
+    bf16, f32 = jnp.bfloat16, jnp.float32
+    replica = lax.axis_index(DP)
+    own_index = lax.axis_index(EXPERT)
+    quarter = lax.axis_index(TENSOR)
+    chosen, _ = migration_slot(swap_list, per_dev)
+    core, chip, base = own_index % 2, own_index // 2, own_index * per_dev
+    info = jnp.stack([chosen, 1 - chosen, core, chip, base, replica, quarter]).astype(jnp.int32)
+
+    ids = jnp.pad(
+        expert_ids.astype(bf16), ((0, 0), (0, IDS_COLS - expert_ids.shape[1])), constant_values=-1
+    )
+    rows = jnp.concatenate([tokens, ids], axis=1)
+    sizes = (hidden_units // 3,) * 3
+    starts = tuple(p * sizes[0] for p in range(3))
+
+    def grad_slice(expert):
+        return lax.dynamic_index_in_dim(hidden_grad[0], expert, 0, keepdims=False)
+
+    leave_grad, stay_grad = grad_slice(chosen), grad_slice(1 - chosen)
+    leave_weight = [
+        lax.dynamic_slice(weights, (replica, chosen, start, 0), (1, 1, size, width))[0, 0]
+        for start, size in zip(starts, sizes)
+    ]
+
+    half = row_count // 2
+    low = lax.dynamic_slice_in_dim(rows, quarter * half, half, 0)
+    low = flip(low, DP, 1)
+    high = flip(low, TENSOR, 1)
+    early = (info, stay_grad, leave_grad, *leave_weight)
+    own_pieces = gather_plane([gather_chips(rows, early=early)])
+    other_pieces = gather_plane([gather_chips(low), gather_chips(high, direct=True)])
+
+    leave_other = flip(after(leave_grad, low), DP, 1)
+    stay_other = flip(after(stay_grad, leave_other), DP, 1)
+    gates = (own_pieces[2][0], other_pieces[2][0], other_pieces[3][1])
+    weight_parts = [
+        flip(after(piece, gate), EXPERT, Y_BIT)
+        for piece, gate in zip(leave_weight, gates)
+    ]
+
+    wide = rows.shape[1]
+    at_chip = lambda k, info: jnp.bitwise_xor(info[3], k)
+    pair = 2 * row_count
+    flat_rows = chips * pair
+    matmul = 2 * per_dev * hidden_units * width * flat_rows * 2
+    once = pl.Buffered(1)
+    any_spec = pl.BlockSpec(memory_space=pl.ANY)
+    rows_spec = pl.BlockSpec((pair, wide), lambda k, info: (k, 0))
+    rows_shape = jax.ShapeDtypeStruct((flat_rows, wide), bf16)
+
+    def piece_call(kernel, pieces, in_specs, out_specs, out_shape, flops):
+        count = len(pieces[0])
+
+        def body(info, *refs):
+            grid = [list(refs[i * count : (i + 1) * count]) for i in range(chips)]
+            kernel(grid, info, *refs[chips * count :])
+
+        run = call(
+            body,
+            (chips,),
+            [any_spec] * (chips * count) + in_specs,
+            out_specs + [rows_spec],
+            out_shape + [rows_shape],
+            flops,
+            20 << 20,
+            [pltpu.VMEM((2, pair, wide), bf16), pltpu.SemaphoreType.DMA((2, count))],
+        )
+        return lambda info, *args: run(info, *[p for group in pieces for p in group], *args)
+
+    slot_spec = pl.BlockSpec(
+        (1, per_dev, hidden_units, pair), lambda k, info: (0, 0, 0, at_chip(k, info))
+    )
+    weight_spec = pl.BlockSpec(weights.shape, lambda k, info: (0, 0, 0, 0), pipeline_mode=once)
+    own_grad_spec = pl.BlockSpec(
+        (2, per_dev, hidden_units, pair), lambda k, info: (0, 0, 0, k)
+    )
+    hidden, own_grad, own_rows = piece_call(
+        own_kernel,
+        own_pieces,
+        [weight_spec, slot_spec],
+        [slot_spec, own_grad_spec],
+        [
+            jax.ShapeDtypeStruct(hidden_grad.shape, bf16),
+            jax.ShapeDtypeStruct((2, per_dev, hidden_units, flat_rows), bf16),
+        ],
+        matmul,
+    )(info, weights, hidden_grad)
+
+    def other_specs(slot):
+        return [
+            pl.BlockSpec(
+                (2, 1, hidden_units, width),
+                lambda k, info: (0, info[slot], 0, 0),
+                pipeline_mode=once,
+            ),
+            pl.BlockSpec((hidden_units, pair), lambda k, info: (0, at_chip(k, info))),
+        ]
+
+    other_out = pl.BlockSpec((hidden_units, pair), lambda k, info: (0, k))
+    other_shape = jax.ShapeDtypeStruct((hidden_units, flat_rows), bf16)
+    leave_terms, other_rows = piece_call(
+        lambda *refs: first_other_kernel(LEAVE, *refs),
+        other_pieces,
+        other_specs(LEAVE),
+        [other_out],
+        [other_shape],
+        matmul // 2,
+    )(info, weights, leave_other)
+    stay_terms = call(
+        lambda *refs: other_kernel(STAY, *refs),
+        (chips,),
+        [rows_spec] + other_specs(STAY),
+        other_out,
+        other_shape,
+        matmul // 2,
+        9 << 20,
+    )(info, other_rows, weights, stay_other)
+
+    tile = 512
+    tiles = width // tile
+    flat_spec = pl.BlockSpec((flat_rows, tile), lambda j, info: (0, j))
+
+    def update(slot, kernel, grad, states, out_specs, out_shapes):
+        spec_at = lambda lead: pl.BlockSpec(
+            (1, 1, hidden_units, tile), lambda j, info: (lead(info), info[slot], 0, j)
+        )
+        state_spec, half_spec = spec_at(lambda info: 0), spec_at(lambda info: info[5])
+        specs = [
+            pl.BlockSpec(
+                (1, 1, hidden_units, flat_rows),
+                lambda j, info: (info[5], info[slot], 0, 0),
+                pipeline_mode=once,
+            ),
+            pl.BlockSpec((hidden_units, flat_rows), lambda j, info: (0, 0), pipeline_mode=once),
+            flat_spec,
+            flat_spec,
+            state_spec,
+            state_spec,
+            half_spec,
+        ]
+        return call(
+            kernel,
+            (tiles,),
+            specs[: 4 + len(states)],
+            out_specs or [state_spec] * len(out_shapes),
+            out_shapes,
+            matmul // 2,
+            18 << 20,
+            grant=VMEM_GRANT if slot == LEAVE else STAY_GRANT,
+        )(info, own_grad, grad, own_rows, other_rows, *states)
+
+    sent = update(
+        LEAVE,
+        leaving_kernel,
+        leave_terms,
+        (first_moment, second_moment),
+        [pl.BlockSpec((n, tile), lambda j, info: (0, j)) for n in sizes for _ in range(2)],
+        [jax.ShapeDtypeStruct((n, width), bf16) for n in sizes for _ in range(2)],
+    )
+    first_in, second_in = [], []
+    for p in range(len(sizes)):
+        pair_out = sent[2 * p : 2 * p + 2]
+        if p > 1:
+            pair_out = [after(piece, second_in[0]) for piece in pair_out]
+        first_in.append(flip(pair_out[0], EXPERT, Y_BIT))
+        second_in.append(flip(pair_out[1], EXPERT, Y_BIT))
+
+    half_spec = pl.BlockSpec((row_count, width), lambda k, info: (k, 0))
+    ta, tb = call(
+        token_kernel,
+        (chips,),
+        [own_grad_spec, weight_spec],
+        [half_spec] * 2,
+        [jax.ShapeDtypeStruct((flat_rows // 2, width), bf16)] * 2,
+        matmul,
+        20 << 20,
+    )(info, own_grad, weights)
+
+    def pick(value, index):
+        return lax.dynamic_index_in_dim(value, index, value.ndim - 3, keepdims=False)
+
+    def send(value, axis, bit):
+        return flip(value.astype(bf16), axis, bit).astype(f32)
+
+    core_sum = ta.astype(f32) + flip(tb, EXPERT, CORE).astype(f32)
+    core_sum = core_sum.reshape(2, 2, 2, row_count // 2, width)
+    sum_x, sum_z = core_sum[..., : width // 2], core_sum[..., width // 2 :]
+    got_x = send(sum_x[:, 1], EXPERT, X_BIT)
+    got_z = send(pick(sum_z, 1 - quarter), TENSOR, 1)
+    sum_x = sum_x[:, 0] + got_x
+    sum_z = pick(sum_z, quarter) + got_z
+    sum_x = pick(sum_x, quarter) + send(pick(sum_x, 1 - quarter), TENSOR, 1)
+    sum_z = sum_z[:, 0] + send(sum_z[:, 1], EXPERT, X_BIT)
+    total = jnp.concatenate([sum_x, sum_z], axis=-1)
+    token_grad = (total[0] + send(total[1], EXPERT, Y_BIT)).astype(bf16)
+
+    state_shape = jax.ShapeDtypeStruct(first_moment.shape, bf16)
+    stay_states = update(
+        STAY,
+        staying_kernel,
+        stay_terms,
+        (first_moment, second_moment, weights),
+        None,
+        [state_shape] * 3,
+    )
+
+    step_units = hidden_units // 6
+    in_spec = pl.BlockSpec((step_units, width), lambda i, info: (i, 0))
+    states = stay_states
+    weight_parts[-1] = after(weight_parts[-1], token_grad)
+    for p, (start, size) in enumerate(zip(starts, sizes)):
+        out_spec = pl.BlockSpec(
+            (1, 1, step_units, width),
+            lambda i, info, first=start // step_units: (0, info[0], first + i, 0),
+        )
+        states = call(
+            arriving_kernel,
+            (size // step_units,),
+            [any_spec] * 3 + [in_spec] * 3,
+            [out_spec] * 3,
+            [state_shape] * 3,
+            0,
+            5 << 20,
+            input_output_aliases={1: 0, 2: 1, 3: 2},
+        )(info, *states, weight_parts[p], first_in[p], second_in[p])
+    return (hidden, token_grad, *states)
+
+
+def token_layout_fits(tokens, expert_ids, weights, first, second, hidden_grad, swap_list):
+    owners, parts = lax.axis_size(EXPERT), lax.axis_size(TENSOR)
+    return (
+        lax.axis_size(DP) == 2
+        and owners == 8
+        and parts == 2
+        and weights.shape[1] == 2
+        and 2 * swap_list.shape[0] == owners
+        and tokens.shape[0] == 128
+        and hidden_grad.shape[3] == owners * tokens.shape[0]
+        and weights.shape[2] % 384 == 0
+        and tokens.shape[1] % 256 == 0
+    )
+
+
+def plan(*args):
+    if not token_layout_fits(*args):
+        return shards(*args)
+    return fast_shards(*args)
+
+
 def solution(mesh):
     in_specs = (
-        P(("dp", "expert"), None),
-        P(("dp", "expert"), None),
-        P(None, "expert", "tensor", None),
-        P("dp", "expert", "tensor", None),
-        P("dp", "expert", "tensor", None),
-        P("dp", "expert", "tensor", None),
+        P((DP, EXPERT), None),
+        P((DP, EXPERT), None),
+        P(None, EXPERT, TENSOR, None),
+        P(DP, EXPERT, TENSOR, None),
+        P(DP, EXPERT, TENSOR, None),
+        P(DP, EXPERT, TENSOR, None),
         P(),
     )
     out_specs = (
-        P("dp", "expert", "tensor", None),
-        P(("dp", "expert", "tensor"), None),
-        P("dp", "expert", "tensor", None),
-        P("dp", "expert", "tensor", None),
-        P("dp", "expert", "tensor", None),
-    )
-    return jax.shard_map(shards, mesh=mesh, in_specs=in_specs, out_specs=out_specs, check_vma=False)
+        P(DP, EXPERT, TENSOR, None),
+        P((DP, EXPERT, TENSOR), None),
+        P(DP, EXPERT, TENSOR, None),
+        P(DP, EXPERT, TENSOR, None),
+        P(DP, EXPERT, TENSOR, None),
+    )
+    return jax.shard_map(plan, mesh=mesh, in_specs=in_specs, out_specs=out_specs, check_vma=False)

time: 669 us -> 252 us (0.38)
  waiting for transfers between devices: 524 us -> 123 us
  Pallas kernels: 0 us -> 60 us
  matrix products: 52.1 us -> 0 us
  local copies, waits for them, and re-layouts: 39.1 us -> 14.8 us
  starting transfers between devices: 17.2 us -> 41.2 us
  between operations: 16.2 us -> 4.24 us
  other arithmetic: 19.5 us -> 8.11 us
    unnamed x2 -> x0, waiting for transfers between devices: 314 us -> none
    all_to_all x2 -> x0, waiting for transfers between devices: 92.4 us -> none  [the longest x1 92.4 us: shards(): lax.all_to_all(outgoing, 'expert', split_axis=1, concat_axis=1, tiled=True)]
    pallas_call x0 -> x9, Pallas kernels: none -> 60 us  [run(): pl.pallas_call(kernel, grid_spec=pltpu.PrefetchScalarGridSpec(num_scalar_...]
    dot_general x7 -> x0, matrix products: 52.1 us -> none  [the longest x2 24.1 us: grad_rows(): jnp.einsum('esd,ecfs->cefd', routed, part_grad, preferred_element_type=jn...]
    ppermute x4 -> x40, starting transfers between devices: 6.95 us -> 41.2 us  [flip(): lax.ppermute(value, axis, [(i, i ^ mask) for i in range(lax.axis_size(axi...]
    reshape x4 -> x0, local copies, waits for them, and re-layouts: 14 us -> none  [the longest x1 8.27 us: shards(): outgoing.reshape(per_dev, owners, tensor_count * capacity, model_width)]
    all_to_all x2 -> x0, local copies, waits for them, and re-layouts: 11 us -> none  [the longest x1 8.42 us: shards(): lax.all_to_all(outgoing, 'expert', split_axis=1, concat_axis=1, tiled=True)]
    all_to_all x2 -> x0, starting transfers between devices: 10 us -> none  [the longest x1 5.19 us: shards(): lax.all_to_all(outgoing, 'expert', split_axis=1, concat_axis=1, tiled=True)]
  transfers between devices with their start and end apart: 7 -> 40, of which waited for: 5 -> 14; matrix products, arithmetic and copies ran while one was open for 8% -> 5% of each run, Pallas kernels for 0% -> 14%
where the time goes in v2:
time: 252 us
  waiting for transfers between devices  123 us (49%)
  Pallas kernels  60 us (24%)
  starting transfers between devices  41.2 us (16%)
  local copies, waits for them, and re-layouts  14.8 us (6%)
  other arithmetic  8.11 us (3%)
  between operations  4.24 us (2%)
    ppermute x40, waiting for transfers between devices, flip(): lax.ppermute(value, axis, [(i, i ^ mask) for i in range(lax.axis_size(axi...  123 us
    pallas_call x9, Pallas kernels, run(): pl.pallas_call(kernel, grid_spec=pltpu.PrefetchScalarGridSpec(num_scalar_...  60 us
    ppermute x40, starting transfers between devices, flip(): lax.ppermute(value, axis, [(i, i ^ mask) for i in range(lax.axis_size(axi...  41.2 us
    unnamed x48, local copies, waits for them, and re-layouts  8.05 us
  transfers between devices with their start and end apart: 40, of which 14 were waited for; matrix products, arithmetic and copies ran while one was open for 5% of the time, Pallas kernels for 14%

profile of v2, /device:TPU:0, one launch (start us, length us, event | category | flops | bytes accessed | tf_op | source)
XLA Modules:
  0.0 251.6 jit_solution(1615828606788936682)
XLA Ops:
  2.5 3.1 %collective-permute-start.3 = (bf16[128,2176]{1,0:T(8,128)(2,1)S(1)}, bf16[128,2176]{1,0:T(8,128)(2,1)S(1)}, u32[]{:S(2)}, u32[]{:S(2)}) collective-permute-start(bf16[128,2176]{1,0:T(8,128)(2,1)S(1)} %fusion.3.refs_0_), channel_id=1, source_target_pairs={{0,8},{2,10},{4,12},{6,14},{8,0},{10,2},{12,4},{14,6},{1,9},{3,11}... | collective-permute-start | bytes 1671176 | tf_op jit(solution)/shard_map/ppermute | solution.py:160
  5.6 1.5 collective-permute-start.1
  7.1 1.4 add_reduce_fusion
  12.5 2.8 %dynamic-slice_bitcast_fusion = (bf16[384,1024]{1,0:T(8,128)(2,1)}, bf16[384,1024]{1,0:T(8,128)(2,1)}) fusion(bf16[1,2,384,1024]{3,2,1,0:T(8,128)(2,1)} %refs_9_.1, s32[]{:T(128)S(6)} %select_n.73, s32[]{:T(128)S(6)} %select_n.72), kind=kLoop, calls=%fused_computation.11 | loop fusion | bytes 3145736 | tf_op jit(solution)/shard_map/jit(dynamic_index_in_dim)/squeeze | solution.py:402
  15.3 2.6 %dynamic-slice_bitcast_fusion.2 = (bf16[128,2048]{1,0:T(8,128)(2,1)}, bf16[128,2048]{1,0:T(8,128)(2,1)}, bf16[128,2048]{1,0:T(8,128)(2,1)}) fusion(bf16[2,2,384,2048]{3,2,1,0:T(8,128)(2,1)} %w_ref.3, s32[]{:T(128)S(6)} %select_n.74, s32[]{:T(128)S(6)} %select_n.73), kind=kLoop, calls=%fused_computation.27 | loop fusion | bytes 3145736 | tf_op jit(solution)/shard_map/squeeze | solution.py:406
  18.2 1.7 collective-permute-start.5
  20.5 11.6 %collective-permute-done.5.refs_6_ = bf16[128,2176]{1,0:T(8,128)(2,1)S(1)} collective-permute-done((bf16[128,2176]{1,0:T(8,128)(2,1)S(1)}, bf16[128,2176]{1,0:T(8,128)(2,1)S(1)}, u32[]{:S(2)}, u32[]{:S(2)}) %collective-permute-start.5) | collective-permute-done | bytes 557088 | tf_op jit(solution)/shard_map/ppermute | solution.py:160
  32.0 1.9 collective-permute-done.6.refs_7_
  34.0 1.4 copy-done.10
  35.4 13.5 %shard_map.110 = (bf16[1,2,384,1024]{3,2,1,0:T(8,128)(2,1)}, bf16[2,2,384,1024]{3,2,1,0:T(8,128)(2,1)S(1)}, bf16[1024,2176]{1,0:T(8,128)(2,1)S(1)}) custom-call(s32[7]{0:T(128)S(1)} %stack.31.info.refs_0_, bf16[128,2176]{1,0:T(8,128)(2,1)S(1)} %fusion.3.refs_0_, bf16[128,2176]{1,0:T(8,128)(2,1)S(1)} %collective-permute-done.refs_1_, ...), custom_call_target="tpu_custom_call" | custom-call | flops 6442450944 | bytes 20971520 | tf_op jit(solution)/shard_map/pallas_call | solution.py:358
  48.9 9.2 %shard_map.111 = (bf16[512,2048]{1,0:T(8,128)(2,1)S(1)}, bf16[512,2048]{1,0:T(8,128)(2,1)}) custom-call(s32[7]{0:T(128)S(1)} %stack.31.info.refs_0_, bf16[2,2,384,1024]{3,2,1,0:T(8,128)(2,1)S(1)} %get-tuple-element.41.grad_ref.own, bf16[2,2,384,2048]{3,2,1,0:T(8,128)(2,1)S(1)} %copy-done.1), custom_call_target="tpu_custom_call" | custom-call | flops 6442450944 | bytes 20971520 | tf_op jit(solution)/shard_map/pallas_call | solution.py:358
  58.3 2.6 %collective-permute-start.13 = (bf16[64,2176]{1,0:T(8,128)(2,1)S(1)}, bf16[64,2176]{1,0:T(8,128)(2,1)S(1)}, u32[]{:S(2)}, u32[]{:S(2)}) collective-permute-start(bf16[64,2176]{1,0:T(8,128)(2,1)S(1)} %constant_dynamic-slice_fusion), channel_id=1, source_target_pairs={{0,16},{16,0},{1,17},{17,1},{2,18},{18,2},{3,19},{19,3},{4,20},{20... | collective-permute-start | bytes 835592 | tf_op jit(solution)/shard_map/ppermute | solution.py:160
  60.9 13.3 %collective-permute-done.13.refs_0_ = bf16[64,2176]{1,0:T(8,128)(2,1)S(1)} collective-permute-done((bf16[64,2176]{1,0:T(8,128)(2,1)S(1)}, bf16[64,2176]{1,0:T(8,128)(2,1)S(1)}, u32[]{:S(2)}, u32[]{:S(2)}) %collective-permute-start.13) | collective-permute-done | bytes 278560 | tf_op jit(solution)/shard_map/ppermute | solution.py:160
  74.1 1.5 collective-permute-start.21
  75.6 1.5 collective-permute-start.17
  77.1 4.0 %collective-permute-start.14 = (bf16[64,2176]{1,0:T(8,128)(2,1)S(1)}, bf16[64,2176]{1,0:T(8,128)(2,1)}, u32[]{:S(2)}, u32[]{:S(2)}) collective-permute-start(bf16[64,2176]{1,0:T(8,128)(2,1)S(1)} %collective-permute-done.13.refs_0_), channel_id=1, source_target_pairs={{0,1},{1,0},{2,3},{3,2},{4,5},{5,4},{6,7},{7,6},{8,9},{9,8},{10,11... | collective-permute-start | bytes 835592 | tf_op jit(solution)/shard_map/ppermute | solution.py:160
  83.5 1.5 collective-permute-start.25
  85.0 12.1 %collective-permute-done.14.refs_1_ = bf16[64,2176]{1,0:T(8,128)(2,1)} collective-permute-done((bf16[64,2176]{1,0:T(8,128)(2,1)S(1)}, bf16[64,2176]{1,0:T(8,128)(2,1)}, u32[]{:S(2)}, u32[]{:S(2)}) %collective-permute-start.14) | collective-permute-done | bytes 278560 | tf_op jit(solution)/shard_map/ppermute | solution.py:160
  97.1 2.4 collective-permute-start.26
  100.7 5.0 %collective-permute-done.26.refs_13_ = bf16[64,2176]{1,0:T(8,128)(2,1)S(1)} collective-permute-done((bf16[64,2176]{1,0:T(8,128)(2,1)}, bf16[64,2176]{1,0:T(8,128)(2,1)S(1)}, u32[]{:S(2)}, u32[]{:S(2)}) %collective-permute-start.26) | collective-permute-done | bytes 278560 | tf_op jit(solution)/shard_map/ppermute | solution.py:160
  105.7 1.4 collective-permute-start.22
  107.1 3.9 %collective-permute-done.29.refs_17_ = bf16[384,1024]{1,0:T(8,128)(2,1)S(1)} collective-permute-done((bf16[384,1024]{1,0:T(8,128)(2,1)}, bf16[384,1024]{1,0:T(8,128)(2,1)S(1)}, u32[]{:S(2)}, u32[]{:S(2)}) %collective-permute-start.29) | collective-permute-done | bytes 786464 | tf_op jit(solution)/shard_map/ppermute | solution.py:160
  111.1 1.5 collective-permute-start.18
  113.2 5.5 %collective-permute-done.18.refs_5_ = bf16[64,2176]{1,0:T(8,128)(2,1)} collective-permute-done((bf16[64,2176]{1,0:T(8,128)(2,1)}, bf16[64,2176]{1,0:T(8,128)(2,1)}, u32[]{:S(2)}, u32[]{:S(2)}) %collective-permute-start.18) | collective-permute-done | bytes 278560 | tf_op jit(solution)/shard_map/ppermute | solution.py:160
  119.2 2.5 convert_add_fusion
  121.8 1.5 collective-permute-start.31
  123.9 1.6 collective-permute-start.30
  125.4 1.5 collective-permute-start.8
  126.9 2.8 %copy-done.2 = bf16[2,2,384,2048]{3,2,1,0:T(8,128)(2,1)S(1)} copy-done((bf16[2,2,384,2048]{3,2,1,0:T(8,128)(2,1)S(1)}, bf16[2,2,384,2048]{3,2,1,0:T(8,128)(2,1)}, u32[]{:S(2)}) %copy-start.2) | copy-done | bytes 6291480
  130.9 7.7 %shard_map.112 = (bf16[384,1024]{1,0:T(8,128)(2,1)S(1)}, bf16[1024,2176]{1,0:T(8,128)(2,1)S(1)}) custom-call(s32[7]{0:T(128)S(1)} %stack.31.info.refs_0_, bf16[64,2176]{1,0:T(8,128)(2,1)S(1)} %collective-permute-done.13.refs_0_, bf16[64,2176]{1,0:T(8,128)(2,1)} %collective-permute-done.14.refs_1_, bf16[64,2176]{1,0:T(8,128)(2,1)S(1)} %copy-done.14, ...), custom_call_target="tpu_custom_call" | custom-call | flops 3221225472 | bytes 20971520 | tf_op jit(solution)/shard_map/pallas_call | solution.py:358
  138.9 1.6 collective-permute-start.10
  140.5 1.9 copy-done.4
  142.4 7.1 %shard_map.115 = (bf16[128,2048]{1,0:T(8,128)(2,1)S(1)}, bf16[128,2048]{1,0:T(8,128)(2,1)S(1)}, bf16[128,2048]{1,0:T(8,128)(2,1)S(1)}, bf16[128,2048]{1,0:T(8,12...) custom-call(s32[7]{0:T(128)S(1)} %stack.31.info.refs_0_, bf16[2,2,384,1024]{3,2,1,0:T(8,128)(2,1)S(1)} %copy-done.8, ...), custom_call_target="tpu_custom_call" | custom-call | flops 3221225472 | bytes 18874368 | tf_op jit(solution)/shard_map/pallas_call | solution.py:358
  150.4 1.4 fusion.1
  151.9 16.5 %collective-permute-done.10 = bf16[2,2,64,1024]{3,2,0,1:T(8,128)(2,1)S(1)} collective-permute-done((bf16[2,2,64,1024]{3,2,0,1:T(8,128)(2,1)S(1)}, bf16[2,2,64,1024]{3,2,0,1:T(8,128)(2,1)S(1)}, u32[]{:S(2)}, u32[]{:S(2)}) %collective-permute-start.10) | collective-permute-done | bytes 524320 | tf_op jit(solution)/shard_map/ppermute | solution.py:160
  169.3 6.0 %shard_map.113.other = bf16[384,1024]{1,0:T(8,128)(2,1)S(1)} custom-call(s32[7]{0:T(128)S(1)} %stack.31.info.refs_0_, bf16[1024,2176]{1,0:T(8,128)(2,1)S(1)} %get-tuple-element.45.refs_1_.b, bf16[2,2,384,2048]{3,2,1,0:T(8,128)(2,1)S(1)} %bitcast.69, bf16[384,1024]{1,0:T(8,128)(2,1)S(1)} %collective-permute-done.30.refs_3_), custom_call_target="tpu_custom_call" | custom-call | flops 3221225472 | bytes 9437184 | tf_op jit(solution)/shard_map/pallas_call | solution.py:358
  175.4 1.3 collective-permute-start.32
  177.6 1.3 collective-permute-start.36
  179.8 1.2 collective-permute-start.38
  181.1 9.2 %collective-permute-done.32.m_ref = bf16[128,2048]{1,0:T(8,128)(2,1)S(1)} collective-permute-done((bf16[128,2048]{1,0:T(8,128)(2,1)S(1)}, bf16[128,2048]{1,0:T(8,128)(2,1)S(1)}, u32[]{:S(2)}, u32[]{:S(2)}) %collective-permute-start.32) | collective-permute-done | bytes 524320 | tf_op jit(solution)/shard_map/ppermute | solution.py:160
  190.3 1.2 collective-permute-start.39
  191.5 10.0 %collective-permute-done.35.m_ref = bf16[128,2048]{1,0:T(8,128)(2,1)S(1)} collective-permute-done((bf16[128,2048]{1,0:T(8,128)(2,1)S(1)}, bf16[128,2048]{1,0:T(8,128)(2,1)S(1)}, u32[]{:S(2)}, u32[]{:S(2)}) %collective-permute-start.35) | collective-permute-done | bytes 524320 | tf_op jit(solution)/shard_map/ppermute | solution.py:160
  201.5 1.2 collective-permute-start.12
  202.7 10.6 %shard_map.114 = (bf16[1,2,384,2048]{3,2,1,0:T(8,128)(2,1)}, bf16[1,2,384,2048]{3,2,1,0:T(8,128)(2,1)}, bf16[1,2,384,2048]{3,2,1,0:T(8,128)(2,1)}) custom-call(s32[7]{0:T(128)S(1)} %stack.31.info.refs_0_, bf16[2,2,384,1024]{3,2,1,0:T(8,128)(2,1)S(1)} %copy-done.9, bf16[384,1024]{1,0:T(8,128)(2,1)S(1)} %shard_map.113.other, bf16[1024,2176]{1,0:T(8,128)(2,1)} %copy-done.3, ...), custom_call_target="tpu_custom_call" | custom-call | flops 3221225472 | bytes 18874368 | tf_op jit(solution)/shard_map/pallas_call | solution.py:358
  213.3 2.0 shard_map.116
  215.3 2.0 shard_map.117
  217.3 31.6 %collective-permute-done.12 = bf16[64,2048]{1,0:T(8,128)(2,1)S(1)} collective-permute-done((bf16[64,2048]{1,0:T(8,128)(2,1)S(1)}, bf16[64,2048]{1,0:T(8,128)(2,1)S(1)}, u32[]{:S(2)}, u32[]{:S(2)}) %collective-permute-start.12) | collective-permute-done | bytes 262176 | tf_op jit(solution)/shard_map/ppermute | solution.py:160
  249.6 2.0 shard_map.118
  (110 shorter events, 14.9 us)
Async XLA Ops:
  2.5 15.7 %collective-permute-start.3 = (bf16[128,2176]{1,0:T(8,128)(2,1)S(1)}, bf16[128,2176]{1,0:T(8,128)(2,1)S(1)}, u32[]{:S(2)}, u32[]{:S(2)}) collective-permute-start(bf16[128,2176]{1,0:T(8,128)(2,1)S(1)} %fusion.3.refs_0_), channel_id=1, source_target_pairs={{0,8},{2,10},{4,12},{6,14},{8,0},{10,2},{12,4},{14,6},{1,9},{3,11}... | collective-permute-start | bytes 1671176 | tf_op jit(solution)/shard_map/ppermute | solution.py:160
  5.6 14.9 %collective-permute-start.1 = (bf16[128,2176]{1,0:T(8,128)(2,1)S(1)}, bf16[128,2176]{1,0:T(8,128)(2,1)S(1)}, u32[]{:S(2)}, u32[]{:S(2)}) collective-permute-start(bf16[128,2176]{1,0:T(8,128)(2,1)S(1)} %fusion.3.refs_0_), channel_id=1, source_target_pairs={{0,4},{2,6},{4,0},{6,2},{8,12},{10,14},{12,8},{14,10},{1,5},{3,7},... | collective-permute-start | bytes 1671176 | tf_op jit(solution)/shard_map/ppermute | solution.py:160
  12.5 21.5 %copy-start.1 = (bf16[2,2,384,2048]{3,2,1,0:T(8,128)(2,1)S(1)}, bf16[2,2,384,2048]{3,2,1,0:T(8,128)(2,1)}, u32[]{:S(2)}) copy-start(bf16[2,2,384,2048]{3,2,1,0:T(8,128)(2,1)} %w_ref.3) | copy-start | bytes 18874372
  18.2 13.8 %collective-permute-start.5 = (bf16[128,2176]{1,0:T(8,128)(2,1)S(1)}, bf16[128,2176]{1,0:T(8,128)(2,1)S(1)}, u32[]{:S(2)}, u32[]{:S(2)}) collective-permute-start(bf16[128,2176]{1,0:T(8,128)(2,1)S(1)} %collective-permute-done.3.refs_4_), channel_id=1, source_target_pairs={{0,4},{2,6},{4,0},{6,2},{8,12},{10,14},{12,8},{14,10},{1,5},{3,7},... | collective-permute-start | bytes 1671176 | tf_op jit(solution)/shard_map/ppermute | solution.py:160
  19.9 12.1 %collective-permute-start = (bf16[128,2176]{1,0:T(8,128)(2,1)S(1)}, bf16[128,2176]{1,0:T(8,128)(2,1)S(1)}, u32[]{:S(2)}, u32[]{:S(2)}) collective-permute-start(bf16[128,2176]{1,0:T(8,128)(2,1)S(1)} %fusion.3.refs_0_), channel_id=1, source_target_pairs={{0,2},{2,0},{4,6},{6,4},{8,10},{10,8},{12,14},{14,12},{1,3},{3,1},... | collective-permute-start | bytes 1671176 | tf_op jit(solution)/shard_map/ppermute | solution.py:160
  19.9 12.1 %collective-permute-start.4 = (bf16[128,2176]{1,0:T(8,128)(2,1)S(1)}, bf16[128,2176]{1,0:T(8,128)(2,1)S(1)}, u32[]{:S(2)}, u32[]{:S(2)}) collective-permute-start(bf16[128,2176]{1,0:T(8,128)(2,1)S(1)} %collective-permute-done.3.refs_4_), channel_id=1, source_target_pairs={{0,2},{2,0},{4,6},{6,4},{8,10},{10,8},{12,14},{14,12},{1,3},{3,1},... | collective-permute-start | bytes 1671176 | tf_op jit(solution)/shard_map/ppermute | solution.py:160
  20.5 11.6 %collective-permute-start.2 = (bf16[128,2176]{1,0:T(8,128)(2,1)S(1)}, bf16[128,2176]{1,0:T(8,128)(2,1)S(1)}, u32[]{:S(2)}, u32[]{:S(2)}) collective-permute-start(bf16[128,2176]{1,0:T(8,128)(2,1)S(1)} %collective-permute-done.1.refs_2_), channel_id=1, source_target_pairs={{0,2},{2,0},{4,6},{6,4},{8,10},{10,8},{12,14},{14,12},{1,3},{3,1},... | collective-permute-start | bytes 1671176 | tf_op jit(solution)/shard_map/ppermute | solution.py:160
  32.0 2.0 collective-permute-start.6
  58.1 60.6 %collective-permute-start.7 = (bf16[512,2048]{1,0:T(8,128)(2,1)}, bf16[512,2048]{1,0:T(8,128)(2,1)}, u32[]{:S(2)}, u32[]{:S(2)}) collective-permute-start(bf16[512,2048]{1,0:T(8,128)(2,1)} %get-tuple-element.43), channel_id=1, source_target_pairs={{0,2},{2,0},{4,6},{6,4},{8,10},{10,8},{12,14},{14,12},{1,3},{3,1},... | collective-permute-start | bytes 6291464 | tf_op jit(solution)/shard_map/ppermute | solution.py:160
  58.3 15.9 %collective-permute-start.13 = (bf16[64,2176]{1,0:T(8,128)(2,1)S(1)}, bf16[64,2176]{1,0:T(8,128)(2,1)S(1)}, u32[]{:S(2)}, u32[]{:S(2)}) collective-permute-start(bf16[64,2176]{1,0:T(8,128)(2,1)S(1)} %constant_dynamic-slice_fusion), channel_id=1, source_target_pairs={{0,16},{16,0},{1,17},{17,1},{2,18},{18,2},{3,19},{19,3},{4,20},{20... | collective-permute-start | bytes 835592 | tf_op jit(solution)/shard_map/ppermute | solution.py:160
  74.1 36.9 %collective-permute-start.29 = (bf16[384,1024]{1,0:T(8,128)(2,1)}, bf16[384,1024]{1,0:T(8,128)(2,1)S(1)}, u32[]{:S(2)}, u32[]{:S(2)}) collective-permute-start(bf16[384,1024]{1,0:T(8,128)(2,1)} %get-tuple-element.44), channel_id=1, source_target_pairs={{0,16},{16,0},{1,17},{17,1},{2,18},{18,2},{3,19},{19,3},{4,20},{20... | collective-permute-start | bytes 2359304 | tf_op jit(solution)/shard_map/ppermute | solution.py:160
  74.1 8.2 %collective-permute-start.21 = (bf16[64,2176]{1,0:T(8,128)(2,1)S(1)}, bf16[64,2176]{1,0:T(8,128)(2,1)}, u32[]{:S(2)}, u32[]{:S(2)}) collective-permute-start(bf16[64,2176]{1,0:T(8,128)(2,1)S(1)} %collective-permute-done.13.refs_0_), channel_id=1, source_target_pairs={{0,8},{2,10},{4,12},{6,14},{8,0},{10,2},{12,4},{14,6},{1,9},{3,11}... | collective-permute-start | bytes 835592 | tf_op jit(solution)/shard_map/ppermute | solution.py:160
  75.6 7.9 %collective-permute-start.17 = (bf16[64,2176]{1,0:T(8,128)(2,1)S(1)}, bf16[64,2176]{1,0:T(8,128)(2,1)}, u32[]{:S(2)}, u32[]{:S(2)}) collective-permute-start(bf16[64,2176]{1,0:T(8,128)(2,1)S(1)} %collective-permute-done.13.refs_0_), channel_id=1, source_target_pairs={{0,4},{2,6},{4,0},{6,2},{8,12},{10,14},{12,8},{14,10},{1,5},{3,7},... | collective-permute-start | bytes 835592 | tf_op jit(solution)/shard_map/ppermute | solution.py:160
  77.1 20.0 %collective-permute-start.14 = (bf16[64,2176]{1,0:T(8,128)(2,1)S(1)}, bf16[64,2176]{1,0:T(8,128)(2,1)}, u32[]{:S(2)}, u32[]{:S(2)}) collective-permute-start(bf16[64,2176]{1,0:T(8,128)(2,1)S(1)} %collective-permute-done.13.refs_0_), channel_id=1, source_target_pairs={{0,1},{1,0},{2,3},{3,2},{4,5},{5,4},{6,7},{7,6},{8,9},{9,8},{10,11... | collective-permute-start | bytes 835592 | tf_op jit(solution)/shard_map/ppermute | solution.py:160
  82.3 17.2 %collective-permute-start.15 = (bf16[64,2176]{1,0:T(8,128)(2,1)S(1)}, bf16[64,2176]{1,0:T(8,128)(2,1)S(1)}, u32[]{:S(2)}, u32[]{:S(2)}) collective-permute-start(bf16[64,2176]{1,0:T(8,128)(2,1)S(1)} %collective-permute-done.13.refs_0_), channel_id=1, source_target_pairs={{0,2},{2,0},{4,6},{6,4},{8,10},{10,8},{12,14},{14,12},{1,3},{3,1},... | collective-permute-start | bytes 835592 | tf_op jit(solution)/shard_map/ppermute | solution.py:160
  83.5 16.8 %collective-permute-start.25 = (bf16[64,2176]{1,0:T(8,128)(2,1)}, bf16[64,2176]{1,0:T(8,128)(2,1)S(1)}, u32[]{:S(2)}, u32[]{:S(2)}) collective-permute-start(bf16[64,2176]{1,0:T(8,128)(2,1)} %collective-permute-done.21.refs_8_), channel_id=1, source_target_pairs={{0,4},{2,6},{4,0},{6,2},{8,12},{10,14},{12,8},{14,10},{1,5},{3,7},... | collective-permute-start | bytes 835592 | tf_op jit(solution)/shard_map/ppermute | solution.py:160
  97.1 8.6 %collective-permute-start.26 = (bf16[64,2176]{1,0:T(8,128)(2,1)}, bf16[64,2176]{1,0:T(8,128)(2,1)S(1)}, u32[]{:S(2)}, u32[]{:S(2)}) collective-permute-start(bf16[64,2176]{1,0:T(8,128)(2,1)} %collective-permute-done.14.refs_1_), channel_id=1, source_target_pairs={{0,12},{2,14},{4,8},{6,10},{8,4},{10,6},{12,0},{14,2},{1,13},{3,15... | collective-permute-start | bytes 835592 | tf_op jit(solution)/shard_map/ppermute | solution.py:160
  100.2 12.3 %collective-permute-start.23 = (bf16[64,2176]{1,0:T(8,128)(2,1)}, bf16[64,2176]{1,0:T(8,128)(2,1)}, u32[]{:S(2)}, u32[]{:S(2)}) collective-permute-start(bf16[64,2176]{1,0:T(8,128)(2,1)} %collective-permute-done.21.refs_8_), channel_id=1, source_target_pairs={{0,2},{2,0},{4,6},{6,4},{8,10},{10,8},{12,14},{14,12},{1,3},{3,1},... | collective-permute-start | bytes 835592 | tf_op jit(solution)/shard_map/ppermute | solution.py:160
  100.2 10.8 %copy-start.15 = (bf16[64,2176]{1,0:T(8,128)(2,1)}, bf16[64,2176]{1,0:T(8,128)(2,1)S(1)}, u32[]{:S(2)}) copy-start(bf16[64,2176]{1,0:T(8,128)(2,1)S(1)} %collective-permute-done.25.refs_12_) | copy-start | bytes 835588
  100.2 12.3 %collective-permute-start.19 = (bf16[64,2176]{1,0:T(8,128)(2,1)}, bf16[64,2176]{1,0:T(8,128)(2,1)}, u32[]{:S(2)}, u32[]{:S(2)}) collective-permute-start(bf16[64,2176]{1,0:T(8,128)(2,1)} %collective-permute-done.17.refs_4_), channel_id=1, source_target_pairs={{0,2},{2,0},{4,6},{6,4},{8,10},{10,8},{12,14},{14,12},{1,3},{3,1},... | collective-permute-start | bytes 835592 | tf_op jit(solution)/shard_map/ppermute | solution.py:160
  105.7 7.4 %collective-permute-start.22 = (bf16[64,2176]{1,0:T(8,128)(2,1)}, bf16[64,2176]{1,0:T(8,128)(2,1)}, u32[]{:S(2)}, u32[]{:S(2)}) collective-permute-start(bf16[64,2176]{1,0:T(8,128)(2,1)} %collective-permute-done.14.refs_1_), channel_id=1, source_target_pairs={{0,8},{2,10},{4,12},{6,14},{8,0},{10,2},{12,4},{14,6},{1,9},{3,11}... | collective-permute-start | bytes 835592 | tf_op jit(solution)/shard_map/ppermute | solution.py:160
  111.1 10.6 %copy-start.11 = (bf16[384,1024]{1,0:T(8,128)(2,1)}, bf16[384,1024]{1,0:T(8,128)(2,1)S(1)}, u32[]{:S(2)}) copy-start(bf16[384,1024]{1,0:T(8,128)(2,1)S(1)} %collective-permute-done.29.refs_17_) | copy-start | bytes 2359300
  111.1 7.6 %collective-permute-start.18 = (bf16[64,2176]{1,0:T(8,128)(2,1)}, bf16[64,2176]{1,0:T(8,128)(2,1)}, u32[]{:S(2)}, u32[]{:S(2)}) collective-permute-start(bf16[64,2176]{1,0:T(8,128)(2,1)} %collective-permute-done.14.refs_1_), channel_id=1, source_target_pairs={{0,4},{2,6},{4,0},{6,2},{8,12},{10,14},{12,8},{14,10},{1,5},{3,7},... | collective-permute-start | bytes 835592 | tf_op jit(solution)/shard_map/ppermute | solution.py:160
  112.6 9.2 %collective-permute-start.16 = (bf16[64,2176]{1,0:T(8,128)(2,1)}, bf16[64,2176]{1,0:T(8,128)(2,1)S(1)}, u32[]{:S(2)}, u32[]{:S(2)}) collective-permute-start(bf16[64,2176]{1,0:T(8,128)(2,1)} %collective-permute-done.14.refs_1_), channel_id=1, source_target_pairs={{0,2},{2,0},{4,6},{6,4},{8,10},{10,8},{12,14},{14,12},{1,3},{3,1},... | collective-permute-start | bytes 835592 | tf_op jit(solution)/shard_map/ppermute | solution.py:160
  112.6 11.3 %collective-permute-start.28 = (bf16[64,2176]{1,0:T(8,128)(2,1)}, bf16[64,2176]{1,0:T(8,128)(2,1)S(1)}, u32[]{:S(2)}, u32[]{:S(2)}) collective-permute-start(bf16[64,2176]{1,0:T(8,128)(2,1)} %copy-done.17), channel_id=1, source_target_pairs={{0,2},{2,0},{4,6},{6,4},{8,10},{10,8},{12,14},{14,12},{1,3},{3,1},... | collective-permute-start | bytes 835592 | tf_op jit(solution)/shard_map/ppermute | solution.py:160
  113.1 10.2 %collective-permute-start.27 = (bf16[64,2176]{1,0:T(8,128)(2,1)}, bf16[64,2176]{1,0:T(8,128)(2,1)S(1)}, u32[]{:S(2)}, u32[]{:S(2)}) collective-permute-start(bf16[64,2176]{1,0:T(8,128)(2,1)} %copy-done.15), channel_id=1, source_target_pairs={{0,2},{2,0},{4,6},{6,4},{8,10},{10,8},{12,14},{14,12},{1,3},{3,1},... | collective-permute-start | bytes 835592 | tf_op jit(solution)/shard_map/ppermute | solution.py:160
  118.7 6.8 %collective-permute-start.24 = (bf16[64,2176]{1,0:T(8,128)(2,1)}, bf16[64,2176]{1,0:T(8,128)(2,1)S(1)}, u32[]{:S(2)}, u32[]{:S(2)}) collective-permute-start(bf16[64,2176]{1,0:T(8,128)(2,1)} %collective-permute-done.22.refs_9_), channel_id=1, source_target_pairs={{0,2},{2,0},{4,6},{6,4},{8,10},{10,8},{12,14},{14,12},{1,3},{3,1},... | collective-permute-start | bytes 835592 | tf_op jit(solution)/shard_map/ppermute | solution.py:160
  118.7 8.2 %collective-permute-start.20 = (bf16[64,2176]{1,0:T(8,128)(2,1)}, bf16[64,2176]{1,0:T(8,128)(2,1)S(1)}, u32[]{:S(2)}, u32[]{:S(2)}) collective-permute-start(bf16[64,2176]{1,0:T(8,128)(2,1)} %collective-permute-done.18.refs_5_), channel_id=1, source_target_pairs={{0,2},{2,0},{4,6},{6,4},{8,10},{10,8},{12,14},{14,12},{1,3},{3,1},... | collective-permute-start | bytes 835592 | tf_op jit(solution)/shard_map/ppermute | solution.py:160
  121.7 16.9 %copy-start.19 = (f32[512,2048]{1,0:T(8,128)}, f32[512,2048]{1,0:T(8,128)S(1)}, u32[]{:S(2)}) copy-start(f32[512,2048]{1,0:T(8,128)S(1)} %convert_add_fusion) | copy-start | bytes 12582916
  121.8 57.2 %collective-permute-start.31 = (bf16[128,2048]{1,0:T(8,128)(2,1)}, bf16[128,2048]{1,0:T(8,128)(2,1)S(1)}, u32[]{:S(2)}, u32[]{:S(2)}) collective-permute-start(bf16[128,2048]{1,0:T(8,128)(2,1)} %get-tuple-element.51), channel_id=1, source_target_pairs={{0,8},{2,10},{4,12},{6,14},{8,0},{10,2},{12,4},{14,6},{1,9},{3,11}... | collective-permute-start | bytes 1572872 | tf_op jit(solution)/shard_map/ppermute | solution.py:160
  123.3 56.6 %collective-permute-start.34 = (bf16[128,2048]{1,0:T(8,128)(2,1)}, bf16[128,2048]{1,0:T(8,128)(2,1)S(1)}, u32[]{:S(2)}, u32[]{:S(2)}) collective-permute-start(bf16[128,2048]{1,0:T(8,128)(2,1)} %get-tuple-element.58), channel_id=1, source_target_pairs={{0,8},{2,10},{4,12},{6,14},{8,0},{10,2},{12,4},{14,6},{1,9},{3,11}... | collective-permute-start | bytes 1572872 | tf_op jit(solution)/shard_map/ppermute | solution.py:160
  123.9 44.8 %collective-permute-start.30 = (bf16[384,1024]{1,0:T(8,128)(2,1)S(1)}, bf16[384,1024]{1,0:T(8,128)(2,1)S(1)}, u32[]{:S(2)}, u32[]{:S(2)}) collective-permute-start(bf16[384,1024]{1,0:T(8,128)(2,1)S(1)} %copy-done.20), channel_id=1, source_target_pairs={{0,16},{16,0},{1,17},{17,1},{2,18},{18,2},{3,19},{19,3},{4,20},{20... | collective-permute-start | bytes 2359304 | tf_op jit(solution)/shard_map/ppermute | solution.py:160
  125.4 24.1 %collective-permute-start.8 = (bf16[2,2,64,1024]{3,2,0,1:T(8,128)(2,1)S(1)}, bf16[2,2,64,1024]{3,2,0,1:T(8,128)(2,1)S(1)}, u32[]{:S(2)}, u32[]{:S(2)}) collective-permute-start(bf16[2,2,64,1024]{3,2,0,1:T(8,128)(2,1)S(1)} %fusion.9), channel_id=1, source_target_pairs={{0,4},{2,6},{4,0},{6,2},{8,12},{10,14},{12,8},{14,10},{1,5},{3,7},... | collective-permute-start | bytes 1572872 | tf_op jit(solution)/shard_map/ppermute | solution.py:160
  138.5 30.8 %copy-start = (bf16[1024,2176]{1,0:T(8,128)(2,1)}, bf16[1024,2176]{1,0:T(8,128)(2,1)S(1)}, u32[]{:S(2)}) copy-start(bf16[1024,2176]{1,0:T(8,128)(2,1)S(1)} %get-tuple-element.45.refs_1_.b) | copy-start | bytes 13369348
  138.9 29.6 %collective-permute-start.10 = (bf16[2,2,64,1024]{3,2,0,1:T(8,128)(2,1)S(1)}, bf16[2,2,64,1024]{3,2,0,1:T(8,128)(2,1)S(1)}, u32[]{:S(2)}, u32[]{:S(2)}) collective-permute-start(bf16[2,2,64,1024]{3,2,0,1:T(8,128)(2,1)S(1)} %fusion.4), channel_id=1, source_target_pairs={{0,1},{1,0},{2,3},{3,2},{4,5},{5,4},{6,7},{7,6},{8,9},{9,8},{10,11... | collective-permute-start | bytes 1572872 | tf_op jit(solution)/shard_map/ppermute | solution.py:160
  140.5 28.8 %slice-start = ((s8[6291456]{0:T(1024)(128)(4,1)}), s8[4194304]{0:T(1024)(128)(4,1)S(1)}, s32[]{:S(2)}) async-start(s8[6291456]{0:T(1024)(128)(4,1)} %bitcast.68), calls=%async_computation | async-start | bytes 8388608
  142.4 26.9 %slice-start.1 = ((s8[6291456]{0:T(1024)(128)(4,1)}), s8[2097152]{0:T(1024)(128)(4,1)S(1)}, s32[]{:S(2)}) async-start(s8[6291456]{0:T(1024)(128)(4,1)} %bitcast.68), calls=%async_computation.1 | async-start | bytes 4194304
  149.5 25.8 %collective-permute-start.33 = (bf16[128,2048]{1,0:T(8,128)(2,1)S(1)}, bf16[128,2048]{1,0:T(8,128)(2,1)S(1)}, u32[]{:S(2)}, u32[]{:S(2)}) collective-permute-start(bf16[128,2048]{1,0:T(8,128)(2,1)S(1)} %get-tuple-element.54), channel_id=1, source_target_pairs={{0,8},{2,10},{4,12},{6,14},{8,0},{10,2},{12,4},{14,6},{1,9},{3,11}... | collective-permute-start | bytes 1572872 | tf_op jit(solution)/shard_map/ppermute | solution.py:160
  168.4 8.3 %collective-permute-start.9 = (bf16[2,64,1024]{2,1,0:T(8,128)(2,1)S(1)}, bf16[2,64,1024]{2,1,0:T(8,128)(2,1)S(1)}, u32[]{:S(2)}, u32[]{:S(2)}) collective-permute-start(bf16[2,64,1024]{2,1,0:T(8,128)(2,1)S(1)} %fusion.12), channel_id=1, source_target_pairs={{0,1},{1,0},{2,3},{3,2},{4,5},{5,4},{6,7},{7,6},{8,9},{9,8},{10,11... | collective-permute-start | bytes 786440 | tf_op jit(solution)/shard_map/ppermute | solution.py:160
  168.7 8.9 %collective-permute-start.11 = (bf16[2,64,1024]{2,1,0:T(8,128)(2,1)S(1)}, bf16[2,64,1024]{2,1,0:T(8,128)(2,1)S(1)}, u32[]{:S(2)}, u32[]{:S(2)}) collective-permute-start(bf16[2,64,1024]{2,1,0:T(8,128)(2,1)S(1)} %fusion.13), channel_id=1, source_target_pairs={{0,4},{2,6},{4,0},{6,2},{8,12},{10,14},{12,8},{14,10},{1,5},{3,7},... | collective-permute-start | bytes 786440 | tf_op jit(solution)/shard_map/ppermute | solution.py:160
  175.4 27.4 %copy-start.9 = (bf16[2,2,384,1024]{3,2,1,0:T(8,128)(2,1)S(1)}, bf16[2,2,384,1024]{3,2,1,0:T(8,128)(2,1)}, u32[]{:S(2)}) copy-start(bf16[2,2,384,1024]{3,2,1,0:T(8,128)(2,1)} %copy-done.7) | copy-start | bytes 9437188
  175.4 14.9 %collective-permute-start.32 = (bf16[128,2048]{1,0:T(8,128)(2,1)S(1)}, bf16[128,2048]{1,0:T(8,128)(2,1)S(1)}, u32[]{:S(2)}, u32[]{:S(2)}) collective-permute-start(bf16[128,2048]{1,0:T(8,128)(2,1)S(1)} %get-tuple-element.53), channel_id=1, source_target_pairs={{0,8},{2,10},{4,12},{6,14},{8,0},{10,2},{12,4},{14,6},{1,9},{3,11}... | collective-permute-start | bytes 1572872 | tf_op jit(solution)/shard_map/ppermute | solution.py:160
  176.7 24.8 %collective-permute-start.35 = (bf16[128,2048]{1,0:T(8,128)(2,1)S(1)}, bf16[128,2048]{1,0:T(8,128)(2,1)S(1)}, u32[]{:S(2)}, u32[]{:S(2)}) collective-permute-start(bf16[128,2048]{1,0:T(8,128)(2,1)S(1)} %get-tuple-element.59), channel_id=1, source_target_pairs={{0,8},{2,10},{4,12},{6,14},{8,0},{10,2},{12,4},{14,6},{1,9},{3,11}... | collective-permute-start | bytes 1572872 | tf_op jit(solution)/shard_map/ppermute | solution.py:160
  177.6 37.7 %collective-permute-start.36 = (bf16[128,2048]{1,0:T(8,128)(2,1)}, bf16[128,2048]{1,0:T(8,128)(2,1)S(1)}, u32[]{:S(2)}, u32[]{:S(2)}) collective-permute-start(bf16[128,2048]{1,0:T(8,128)(2,1)} %get-tuple-element.60), channel_id=1, source_target_pairs={{0,8},{2,10},{4,12},{6,14},{8,0},{10,2},{12,4},{14,6},{1,9},{3,11}... | collective-permute-start | bytes 1572872 | tf_op jit(solution)/shard_map/ppermute | solution.py:160
  179.0 70.6 %collective-permute-start.37 = (bf16[128,2048]{1,0:T(8,128)(2,1)S(1)}, bf16[128,2048]{1,0:T(8,128)(2,1)S(1)}, u32[]{:S(2)}, u32[]{:S(2)}) collective-permute-start(bf16[128,2048]{1,0:T(8,128)(2,1)S(1)} %copy-done.21), channel_id=1, source_target_pairs={{0,8},{2,10},{4,12},{6,14},{8,0},{10,2},{12,4},{14,6},{1,9},{3,11}... | collective-permute-start | bytes 1572872 | tf_op jit(solution)/shard_map/ppermute | solution.py:160
  179.8 69.8 %collective-permute-start.38 = (bf16[128,2048]{1,0:T(8,128)(2,1)}, bf16[128,2048]{1,0:T(8,128)(2,1)S(1)}, u32[]{:S(2)}, u32[]{:S(2)}) collective-permute-start(bf16[128,2048]{1,0:T(8,128)(2,1)} %get-tuple-element.67), channel_id=1, source_target_pairs={{0,8},{2,10},{4,12},{6,14},{8,0},{10,2},{12,4},{14,6},{1,9},{3,11}... | collective-permute-start | bytes 1572872 | tf_op jit(solution)/shard_map/ppermute | solution.py:160
  190.3 59.3 %collective-permute-start.39 = (bf16[128,2048]{1,0:T(8,128)(2,1)}, bf16[128,2048]{1,0:T(8,128)(2,1)S(1)}, u32[]{:S(2)}, u32[]{:S(2)}) collective-permute-start(bf16[128,2048]{1,0:T(8,128)(2,1)} %get-tuple-element.69), channel_id=1, source_target_pairs={{0,8},{2,10},{4,12},{6,14},{8,0},{10,2},{12,4},{14,6},{1,9},{3,11}... | collective-permute-start | bytes 1572872 | tf_op jit(solution)/shard_map/ppermute | solution.py:160
  201.5 47.3 %collective-permute-start.12 = (bf16[64,2048]{1,0:T(8,128)(2,1)S(1)}, bf16[64,2048]{1,0:T(8,128)(2,1)S(1)}, u32[]{:S(2)}, u32[]{:S(2)}) collective-permute-start(bf16[64,2048]{1,0:T(8,128)(2,1)S(1)} %fusion.14), channel_id=1, source_target_pairs={{0,8},{2,10},{4,12},{6,14},{8,0},{10,2},{12,4},{14,6},{1,9},{3,11}... | collective-permute-start | bytes 786440 | tf_op jit(solution)/shard_map/ppermute | solution.py:160
  (16 other events, 94.1 us)
